TPU v7x, 32 devices: a whole 2x2x4 slice. The times are simulated.
32 devices in a mesh: grid: 2 (over x), row: 4 (over y, core), col: 4 (over z).
Axes of the slice: x: 2, y: 2, z: 4, core: 2. Of those that a mesh axis runs over, the one named last changes fastest.
Arguments:
- rhs_in: bfloat16 [32768, 1024], P(('grid', 'row', 'col')), may hold values from -6 to 6
- rhs_target: int32 [32768], P(('grid', 'row', 'col')), may hold values from 0 to 32767, as said below
- leaf_inverse: bfloat16 [64, 512, 512], P(('grid', 'row', 'col')), may hold values from -0.25 to 0.25
- level_one_blocks: bfloat16 [2, 4, 4, 4, 2, 512, 512], P('grid', 'row', 'col'), may hold values from -0.0625 to 0.0625
- level_one_pattern: int32 [2, 4, 4, 4, 2], P('grid', 'row', 'col'), may hold values 0 or 1
- level_one_rhs: bfloat16 [2, 4, 512, 1024], P('grid', 'row', None, 'col'), may hold values from -6 to 6
- level_one_inverse: bfloat16 [2, 4, 512, 512], P('grid', 'row'), may hold values from -0.25 to 0.25
- top_blocks: bfloat16 [2, 4, 4, 512, 512], P('grid', 'row'), may hold values from -0.09375 to 0.09375
- top_rhs: bfloat16 [4, 512, 1024], P(None, None, 'col'), may hold values from -6 to 6
- top_inverse: bfloat16 [4, 512, 512], replicated, may hold values from -0.25 to 0.25
- top_chain: bfloat16 [6, 512, 512], replicated, may hold values from -0.125 to 0.125
Outputs:
- leaf_solution: bfloat16 [32768, 1024], P(('grid', 'row', 'col'))
- level_one_solution: bfloat16 [2, 4, 512, 1024], P('grid', 'row', None, 'col')
- top_solution: bfloat16 [4, 512, 1024], P(None, None, 'col')
Inputs may be any that keep to these rules, and one draw needn't show every extreme that they name: rhs_target is a permutation; position p belongs to the device of flat index p // 1024 over grid, row, col (grid slowest); the 1024 arrival rows of every device go exactly 32 to each device.
All inputs are finite; a program needn't handle non-finite values. No bound on the sum of `level_one_pattern` on one device may be relied on, other than what follows from the above.
Results may differ from a plain program's by a relative error of at most 0.02.
Values may be sent and summed in bfloat16 or wider, within the bound.
A program may use at most 128 MiB of HBM per device.

v0:
```python
import jax
import jax.numpy as jnp
from jax import lax
from jax.sharding import PartitionSpec as P


def forward_chain(top_rhs, totals, top_inverse, top_chain):
    solved = []
    for current in range(top_inverse.shape[0]):
        running = top_rhs[current].astype(jnp.float32) - totals[current]
        for earlier in range(current):
            running = running - jnp.dot(
                top_chain[current * (current - 1) // 2 + earlier],
                solved[earlier],
                preferred_element_type=jnp.float32,
            )
        solved.append(
            jnp.dot(
                top_inverse[current],
                running.astype(jnp.bfloat16),
                preferred_element_type=jnp.float32,
            ).astype(jnp.bfloat16)
        )
    return jnp.stack(solved)


def shards(
    rhs_in,
    rhs_target,
    leaf_inverse,
    level_one_blocks,
    level_one_pattern,
    level_one_rhs,
    level_one_inverse,
    top_blocks,
    top_rhs,
    top_inverse,
    top_chain,
):
    device_count = lax.axis_size(("grid", "row", "col"))
    rows_local, rhs_width = rhs_in.shape
    share_rows = rows_local // device_count
    destination = rhs_target // rows_local
    ordering = jnp.argsort(destination, stable=True)
    send_rows = rhs_in[ordering].reshape(device_count, share_rows, rhs_width)
    send_places = (rhs_target % rows_local)[ordering].reshape(device_count, share_rows)
    got_rows, got_places = (
        lax.all_to_all(send_rows, ("grid", "row", "col"), split_axis=0, concat_axis=0, tiled=True),
        lax.all_to_all(
            send_places, ("grid", "row", "col"), split_axis=0, concat_axis=0, tiled=True
        ),
    )
    placed = got_rows.reshape(rows_local, rhs_width)[jnp.argsort(got_places.reshape(rows_local))]
    leaf_count, block_size = (leaf_inverse.shape[0], leaf_inverse.shape[1])
    leaf_rhs = placed.reshape(leaf_count, block_size, rhs_width)
    leaf_solution = jnp.einsum(
        "lij,ljr->lir", leaf_inverse, leaf_rhs, preferred_element_type=jnp.float32
    ).astype(jnp.bfloat16)
    blocks = level_one_blocks[0, 0, 0]
    pattern = level_one_pattern[0, 0, 0]
    present = pattern.astype(jnp.bfloat16)
    masked = (
        lax.all_gather(leaf_solution[None], "row", axis=0, tiled=True) * present[:, :, None, None]
    )
    partial_sum = jnp.einsum("nlij,nljr->ir", blocks, masked, preferred_element_type=jnp.float32)
    update_one = lax.psum_scatter(
        partial_sum.astype(jnp.bfloat16), "col", scatter_dimension=1, tiled=True
    ).astype(jnp.float32)
    resid_one = (level_one_rhs[0, 0].astype(jnp.float32) - update_one).astype(jnp.bfloat16)
    solution_one = jnp.dot(
        level_one_inverse[0, 0], resid_one, preferred_element_type=jnp.float32
    ).astype(jnp.bfloat16)
    top_terms = jnp.einsum(
        "tij,jr->tir", top_blocks[0, 0], solution_one, preferred_element_type=jnp.float32
    )
    shares = lax.psum_scatter(
        top_terms.astype(jnp.bfloat16), ("grid", "row"), scatter_dimension=2, tiled=True
    ).astype(jnp.float32)
    piece_width = shares.shape[2]
    offset = lax.axis_index(("grid", "row")) * piece_width
    rhs_piece = lax.dynamic_slice_in_dim(top_rhs, offset, piece_width, 2)
    solved_piece = forward_chain(rhs_piece, shares, top_inverse, top_chain)
    top_solution = lax.all_gather(solved_piece, ("grid", "row"), axis=2, tiled=True)
    return (leaf_solution.reshape(rows_local, rhs_width), solution_one[None, None], top_solution)


def solution(mesh):
    in_specs = (
        P(("grid", "row", "col"), None),
        P(("grid", "row", "col")),
        P(("grid", "row", "col"), None, None),
        P("grid", "row", "col", None, None, None, None),
        P("grid", "row", "col", None, None),
        P("grid", "row", None, "col"),
        P("grid", "row", None, None),
        P("grid", "row", None, None, None),
        P(None, None, "col"),
        P(),
        P(),
    )
    out_specs = (
        P(("grid", "row", "col"), None),
        P("grid", "row", None, "col"),
        P(None, None, "col"),
    )
    return jax.shard_map(shards, mesh=mesh, in_specs=in_specs, out_specs=out_specs, check_vma=False)
```

profile of v0, /device:TPU:17, one launch (start us, length us, event | category | flops | bytes accessed | tf_op | source)
XLA Modules:
  0.0 285.1 jit_solution(2062001286280841664)
XLA Ops:
  8.0 4.4 %sort.34 = (s32[1024]{0:T(1024)}, s32[1024]{0:T(1024)S(1)}) sort(s32[1024]{0:T(1024)S(1)} %get-tuple-element.21, s32[1024]{0:T(1024)S(1)} %iota.8), dimensions={0}, to_apply=%region_0.1 | sort | flops 10240 | bytes 16384 | tf_op jit(solution)/shard_map/jit(argsort)/sort | solution.py:44
  12.4 4.5 %gather_fusion.1 = s32[1024]{0:T(1024)S(1)} fusion(s32[1024]{0:T(1024)S(1)} %get-tuple-element.20, s32[1024]{0:T(1024)S(1)} %fusion.70), kind=kCustom, calls=%fused_computation.1 | custom fusion | bytes 12288 | tf_op jit(solution)/shard_map/gather | solution.py:46
  17.6 6.2 %all-to-all-start.1 = ((s32[32,1,32]{2,1,0:T(1,128)}), s32[32,1,32]{2,1,0:T(1,128)S(1)}, u32[]{:S(2)}, u32[]{:S(2)}) async-start(s32[32,1,32]{2,1,0:T(1,128)} %all_to_all.10), calls=%async_computation.1 | async-start | bytes 32768 | tf_op jit(solution)/shard_map/all_to_all | solution.py:49
  23.9 5.3 %gather_fusion = bf16[1024,1024]{1,0:T(8,128)(2,1)} fusion(bf16[1024,1024]{1,0:T(8,128)(2,1)S(1)} %copy-done, s32[1024]{0:T(1024)S(1)} %fusion.70), kind=kCustom, calls=%fused_computation | custom fusion | bytes 4198400 | tf_op jit(solution)/shard_map/gather | solution.py:45
  29.2 5.9 %all-to-all-start = ((bf16[32,32,1024]{2,1,0:T(8,128)(2,1)}), bf16[32,32,1024]{2,1,0:T(8,128)(2,1)}, u32[]{:S(2)}, u32[]{:S(2)}) async-start(bf16[32,32,1024]{2,1,0:T(8,128)(2,1)} %bitcast.153), calls=%async_computation | async-start | bytes 4194304 | tf_op jit(solution)/shard_map/all_to_all | solution.py:48
  36.4 4.4 %sort.35 = (s32[1024]{0:T(1024)}, s32[1024]{0:T(1024)S(1)}) sort(s32[1024]{0:T(1024)S(1)} %reshape.43, s32[1024]{0:T(1024)S(1)} %iota.9), dimensions={0}, to_apply=%region_1.2 | sort | flops 10240 | bytes 16384 | tf_op jit(solution)/shard_map/jit(argsort)/sort | solution.py:53
  40.8 41.5 %all-to-all-done = bf16[32,32,1024]{2,1,0:T(8,128)(2,1)} async-done(((bf16[32,32,1024]{2,1,0:T(8,128)(2,1)}), bf16[32,32,1024]{2,1,0:T(8,128)(2,1)}, u32[]{:S(2)}, u32[]{:S(2)}) %all-to-all-start) | async-done | bytes 2097184 | tf_op jit(solution)/shard_map/all_to_all | solution.py:48
  82.3 8.0 %gather_fusion.2 = bf16[1024,1024]{1,0:T(8,128)(2,1)} fusion(bf16[1024,1024]{1,0:T(8,128)(2,1)} %bitcast.1, s32[1024]{0:T(1024)S(1)} %fusion.71), kind=kCustom, calls=%fused_computation.2 | custom fusion | bytes 4198400 | tf_op jit(solution)/shard_map/gather | solution.py:53
  90.3 4.2 %convolution_convert_fusion = bf16[2,1024,512]{1,2,0:T(8,128)(2,1)} fusion(bf16[2,512,512]{2,1,0:T(8,128)(2,1)S(1)} %copy-done.3, bf16[2,512,1024]{2,1,0:T(8,128)(2,1)} %bitcast.156), kind=kOutput, calls=%fused_computation.10 | convolution fusion | flops 1074790400 | bytes 5242880 | tf_op jit(solution)/shard_map/lij,ljr->lir/dot_general | solution.py:56
  95.2 57.3 %all-gather.6.cloned.1.call-done = bf16[8,512,1024]{2,1,0:T(8,128)(2,1)} async-done(((bf16[2,512,1024]{2,1,0:T(8,128)(2,1)}), bf16[8,512,1024]{2,1,0:T(8,128)(2,1)}) %all-gather.6.cloned.1.call-update) | async-done | bytes 8388624 | tf_op jit(solution)/shard_map/all_gather | solution.py:63
  152.5 11.5 %copy.23 = bf16[4,2,512,1024]{2,3,0,1:T(8,128)(2,1)} copy(bf16[4,2,512,1024]{3,2,1,0:T(8,128)(2,1)} %bitcast.154) | data formatting | bytes 16777216 | tf_op jit(solution)/shard_map/all_gather | solution.py:63
  164.1 10.1 %fusion.16 = bf16[512,1024]{0,1:T(8,128)(2,1)} fusion(bf16[4,2,512,1024]{2,3,0,1:T(8,128)(2,1)} %copy.23, bf16[4,2]{0,1:T(2,128)(2,1)S(1)} %convert_bitcast_fusion, bf16[1,1,1,4,2,512,512]{6,5,4,3,2,1,0:T(8,128)(2,1)} %param.14), kind=kOutput, calls=%fused_computation.13 | convolution fusion | flops 4299685888 | bytes 13631504 | tf_op jit(solution)/shard_map/nlij,nljr->ir/dot_general | solution.py:65
  174.4 25.3 %reduce-scatter.3.cloned.1.call-done = bf16[512,256]{0,1:T(8,128)(2,1)} async-done(((bf16[512,1024]{0,1:T(8,128)(2,1)}), bf16[512,256]{0,1:T(8,128)(2,1)}) %reduce-scatter.3.cloned.1.call-update) | async-done | bytes 262160 | tf_op jit(solution)/shard_map/reduce_scatter | solution.py:66
  201.0 3.3 %fusion.13 = bf16[4,512,256]{1,2,0:T(8,128)(2,1)} fusion(bf16[1,1,4,512,512]{4,3,2,1,0:T(8,128)(2,1)} %param.18, bf16[256,512]{1,0:T(8,128)(2,1)S(1)} %convolution_convert_fusion.1), kind=kOutput, calls=%fused_computation.12 | convolution fusion | flops 537395200 | bytes 3407872 | tf_op jit(solution)/shard_map/tij,jr->tir/dot_general | solution.py:73
  204.4 1.3 constant_dynamic-slice_fusion
  206.1 34.1 %reduce-scatter.5.cloned.1.call-done = bf16[4,512,32]{1,2,0:T(8,128)(2,1)} async-done(((bf16[4,512,256]{1,2,0:T(8,128)(2,1)}), bf16[4,512,32]{1,2,0:T(8,128)(2,1)}) %reduce-scatter.5.cloned.1.call-update) | async-done | bytes 131088 | tf_op jit(solution)/shard_map/reduce_scatter | solution.py:76
  242.4 1.3 fusion.23
  243.7 1.6 convolution_convert_fusion.4
  245.3 1.3 fusion.25
  246.6 1.3 fusion.22
  248.0 1.6 convolution_convert_fusion.3
  249.6 1.7 fusion.30
  252.8 23.5 %all-gather.4.cloned.1.call-done = bf16[4,512,256]{1,2,0:T(8,128)(2,1)} async-done(((bf16[4,512,32]{1,2,0:T(8,128)(2,1)}), bf16[4,512,256]{1,2,0:T(8,128)(2,1)}) %all-gather.4.cloned.1.call-update) | async-done | bytes 1048592 | tf_op jit(solution)/shard_map/all_gather | solution.py:83
  276.3 2.3 copy.27
  (39 shorter events, 9.2 us)
Async XLA Ops:
  7.2 16.7 %copy-start = (bf16[1024,1024]{1,0:T(8,128)(2,1)S(1)}, bf16[1024,1024]{1,0:T(8,128)(2,1)}, u32[]{:S(2)}) copy-start(bf16[1024,1024]{1,0:T(8,128)(2,1)} %param.11) | copy-start | bytes 6291460
  17.6 11.6 %all-to-all-start.1 = ((s32[32,1,32]{2,1,0:T(1,128)}), s32[32,1,32]{2,1,0:T(1,128)S(1)}, u32[]{:S(2)}, u32[]{:S(2)}) async-start(s32[32,1,32]{2,1,0:T(1,128)} %all_to_all.10), calls=%async_computation.1 | async-start | bytes 32768 | tf_op jit(solution)/shard_map/all_to_all | solution.py:49
  29.2 53.1 %all-to-all-start = ((bf16[32,32,1024]{2,1,0:T(8,128)(2,1)}), bf16[32,32,1024]{2,1,0:T(8,128)(2,1)}, u32[]{:S(2)}, u32[]{:S(2)}) async-start(bf16[32,32,1024]{2,1,0:T(8,128)(2,1)} %bitcast.153), calls=%async_computation | async-start | bytes 4194304 | tf_op jit(solution)/shard_map/all_to_all | solution.py:48
  35.1 117.4 %all-gather.6.cloned.1.call-start = ((), (), s32[]{:S(2)}) async-start(), calls=%async_computation.7 | async-start | bytes 10485760 | tf_op jit(solution)/shard_map/all_gather | solution.py:63
  82.3 8.0 %copy-start.3 = (bf16[2,512,512]{2,1,0:T(8,128)(2,1)S(1)}, bf16[2,512,512]{2,1,0:T(8,128)(2,1)}, u32[]{:S(2)}) copy-start(bf16[2,512,512]{2,1,0:T(8,128)(2,1)} %param.13) | copy-start | bytes 3145732
  94.5 0.7 copy-start.4
  94.6 105.2 %reduce-scatter.3.cloned.1.call-start = ((), (), s32[]{:S(2)}) async-start(), calls=%async_computation.4 | async-start | bytes 1310720 | tf_op jit(solution)/shard_map/reduce_scatter | solution.py:66
  164.1 10.2 %copy-start.2 = (bf16[1,1,512,256]{3,2,1,0:T(8,128)(2,1)S(1)}, bf16[1,1,512,256]{3,2,1,0:T(8,128)(2,1)}, u32[]{:S(2)}) copy-start(bf16[1,1,512,256]{3,2,1,0:T(8,128)(2,1)} %param.16) | copy-start | bytes 786436
  164.1 35.6 %copy-start.1 = (bf16[1,1,512,512]{3,2,1,0:T(8,128)(2,1)S(1)}, bf16[1,1,512,512]{3,2,1,0:T(8,128)(2,1)}, u32[]{:S(2)}) copy-start(bf16[1,1,512,512]{3,2,1,0:T(8,128)(2,1)} %param.17) | copy-start | bytes 1572868
  174.2 65.9 %reduce-scatter.5.cloned.1.call-start = ((), (), s32[]{:S(2)}) async-start(), calls=%async_computation.5 | async-start | bytes 1179648 | tf_op jit(solution)/shard_map/reduce_scatter | solution.py:76
  204.3 71.9 %all-gather.4.cloned.1.call-start = ((), (), s32[]{:S(2)}) async-start(), calls=%async_computation.6 | async-start | bytes 1179648 | tf_op jit(solution)/shard_map/all_gather | solution.py:83
Sparse Core Ops, SparseCore 0:
  94.7 57.8 all-gather.5
  174.4 25.3 reduce-scatter.2
  204.5 35.6 reduce-scatter.4
  252.1 24.1 all-gather.3
where the time goes:
time: 287 us; the launch traced here: 285 us
  waiting for transfers between devices  182 us (63%)
  local copies, waits for them, and re-layouts  36.2 us (13%)
  matrix products  29.1 us (10%)
  between operations  13.9 us (5%)
  starting transfers between devices  12.3 us (4%)
  other arithmetic  11.9 us (4%)
    all_gather x1, waiting for transfers between devices, shards(): lax.all_gather(leaf_solution[None], 'row', axis=0, tiled=True)  57.3 us
    all_to_all x1, waiting for transfers between devices, shards(): lax.all_to_all(send_rows, ('grid', 'row', 'col'), split_axis=0, concat_ax...  41.5 us
    reduce_scatter x1, waiting for transfers between devices, shards(): lax.psum_scatter(top_terms.astype(jnp.bfloat16), ('grid', 'row'), scatter...  34.1 us
    reduce_scatter x1, waiting for transfers between devices, shards(): lax.psum_scatter(partial_sum.astype(jnp.bfloat16), 'col', scatter_dimensi...  25.3 us
    all_gather x1, waiting for transfers between devices, shards(): lax.all_gather(solved_piece, ('grid', 'row'), axis=2, tiled=True)  23.5 us
    all_gather x1, local copies, waits for them, and re-layouts, shards(): lax.all_gather(leaf_solution[None], 'row', axis=0, tiled=True)  11.5 us
    dot_general x1, matrix products, shards(): jnp.einsum('nlij,nljr->ir', blocks, masked, preferred_element_type=jnp.fl...  10.1 us
    gather x1, local copies, waits for them, and re-layouts, shards(): got_rows.reshape(rows_local, rhs_width)  8.01 us
  transfers between devices with their start and end apart: 6, of which 5 were waited for; matrix products, arithmetic and copies ran while one was open for 5% of the time, Pallas kernels for 0%

commit v1 on v0

v1 whole, which is shorter than its diff:
```python
import functools

import jax
import jax.numpy as jnp
from jax import lax
from jax.experimental import pallas as pl
from jax.experimental.pallas import tpu as pltpu
from jax.sharding import PartitionSpec as P

MESH = pl.DeviceIdType.MESH
VMEM = pl.BlockSpec(memory_space=pltpu.VMEM)
ANY = pl.BlockSpec(memory_space=pl.ANY)


def greet(axes, sizes):
    barrier = pltpu.get_barrier_semaphore()
    total = 1
    for size in sizes:
        total *= size
    flat = 0
    for axis, size in zip(axes, sizes):
        flat = flat * size + lax.axis_index(axis)

    @pl.loop(1, total)
    def _(step):
        rest = lax.rem(flat + step, total)
        coords = {}
        for axis, size in reversed(list(zip(axes, sizes))):
            coords[axis] = lax.rem(rest, size)
            rest = rest // size
        pl.semaphore_signal(barrier, inc=1, device_id=coords, device_id_type=MESH)

    pl.semaphore_wait(barrier, total - 1)


def dot(a, b):
    return jnp.dot(a, b, preferred_element_type=jnp.float32)


def dot_t(a, b):
    return lax.dot_general(a, b, (((1,), (1,)), ((), ())), preferred_element_type=jnp.float32)


def level_one_kernel(
    rows,
    cols,
    sol_ref,
    blocks_ref,
    pattern_ref,
    rhs_ref,
    inverse_ref,
    out_ref,
    gathered,
    other_blocks,
    other_pattern,
    totals,
    pieces,
    landed,
    block_sems,
    pattern_sems,
    gather_send,
    gather_recv,
    piece_send,
    piece_recv,
):
    me = lax.axis_index("row")
    col = lax.axis_index("col")
    side = lax.rem(me, 2)
    mate = me + 1 - 2 * side
    leaves, _, width = sol_ref.shape
    half = width // 2
    half_cols = cols // 2
    share = width // cols

    def row_at(offset):
        pair = lax.rem(me // 2 + offset // 2, rows // 2)
        return pair * 2 + lax.rem(side + offset % 2, 2)

    greet(("row", "col"), (rows, cols))

    def gather_copy(target, owner, leaf):
        begin = pl.multiple_of(lax.rem(target, 2) * half, half)
        return pltpu.make_async_remote_copy(
            src_ref=sol_ref.at[leaf, :, pl.ds(begin, half)],
            dst_ref=gathered.at[owner, leaf],
            send_sem=gather_send.at[target, leaf],
            recv_sem=gather_recv.at[owner, leaf],
            device_id={"row": target},
            device_id_type=MESH,
        )

    for leaf in range(leaves):
        for offset in range(rows - 1, 0, -1):
            if offset != 1:
                gather_copy(row_at(offset), me, leaf).start()
    pattern_copy = pltpu.make_async_remote_copy(
        src_ref=pattern_ref,
        dst_ref=other_pattern,
        send_sem=pattern_sems.at[0],
        recv_sem=pattern_sems.at[1],
        device_id={"row": mate},
        device_id_type=MESH,
    )
    pattern_copy.start()

    def block_copy(owner):
        return pltpu.make_async_remote_copy(
            src_ref=blocks_ref.at[owner],
            dst_ref=other_blocks.at[owner],
            send_sem=block_sems.at[0, owner],
            recv_sem=block_sems.at[1, owner],
            device_id={"row": mate},
            device_id_type=MESH,
        )

    block_copy(mate).start()
    for leaf in range(leaves):
        gather_copy(mate, me, leaf).start()
    for offset in range(1, rows):
        block_copy(row_at(offset - 1 if offset % 2 else offset + 1)).start()
    totals[...] = jnp.zeros_like(totals)
    mine = pl.multiple_of(side * half, half)
    for leaf in range(leaves):
        gathered[me, leaf] = sol_ref[leaf, :, pl.ds(mine, half)]

    def add(which, blocks, pattern, owner, leaf):
        block = blocks[owner, leaf]
        mask = pattern[owner, leaf]
        tall = block.shape[0] // mask.shape[0]
        masked = (block.reshape(tall, *mask.shape) * mask[None]).reshape(block.shape)
        totals[which] += dot(masked, gathered[owner, leaf])

    for leaf in range(leaves):
        add(0, blocks_ref, pattern_ref, me, leaf)
    pattern_copy.wait()

    def meet(offset):
        owner = row_at(offset)
        block_copy(owner).wait()
        for leaf in range(leaves):
            if offset:
                gather_copy(owner, owner, leaf).wait_recv()
                add(0, blocks_ref, pattern_ref, owner, leaf)
            add(1, other_blocks, other_pattern, owner, leaf)

    for offset in range(rows):
        meet(offset)
    for offset in range(1, rows):
        for leaf in range(leaves):
            gather_copy(row_at(offset), me, leaf).wait_send()

    def piece_copy(which, part):
        return pltpu.make_async_remote_copy(
            src_ref=pieces.at[which, part],
            dst_ref=landed.at[col],
            send_sem=piece_send.at[which, part],
            recv_sem=piece_recv.at[col],
            device_id={"row": mate if which else me, "col": side * half_cols + part},
            device_id_type=MESH,
        )

    for part in range(half_cols):
        for which in range(2):
            pieces[which, part] = totals[which, :, part * share : (part + 1) * share].astype(
                pieces.dtype
            )
    for part in range(half_cols):
        for which in range(2):
            stays = (side * half_cols + part == col) if which == 0 else None
            if stays is None:
                piece_copy(which, part).start()
            else:

                @pl.when(jnp.logical_not(stays))
                def _(which=which, part=part):
                    piece_copy(which, part).start()

                @pl.when(stays)
                def _(which=which, part=part):
                    landed[col] = pieces[which, part]

    source_side = col // half_cols
    for step in range(cols):
        source = lax.rem(col + step, cols)
        arrival = pltpu.make_async_remote_copy(
            src_ref=pieces.at[0, 0],
            dst_ref=landed.at[source],
            send_sem=piece_send.at[0, 0],
            recv_sem=piece_recv.at[source],
            device_id={"row": mate},
            device_id_type=MESH,
        )
        if step == 0:

            @pl.when(source_side != side)
            def _():
                arrival.wait_recv()
        else:
            arrival.wait_recv()
    for part in range(half_cols):

        @pl.when(side * half_cols + part != col)
        def _(part=part):
            piece_copy(0, part).wait_send()

        piece_copy(1, part).wait_send()
    update = landed[0].astype(jnp.float32)
    for step in range(1, cols):
        update = update + landed[step].astype(jnp.float32)
    resid = (rhs_ref[...].astype(jnp.float32) - update).astype(jnp.bfloat16)
    out_ref[...] = dot(inverse_ref[...], resid).astype(jnp.bfloat16)


def level_one(sol, blocks, pattern, rhs, inverse):
    rows, cols = lax.axis_size("row"), lax.axis_size("col")
    owners, leaves, size, _ = blocks.shape
    width = sol.shape[2]
    half, share = width // 2, width // cols
    bf16 = jnp.bfloat16
    mask = jnp.broadcast_to(pattern.astype(bf16)[:, :, None, None], (owners, leaves, 16, size))
    dma = pltpu.SemaphoreType.DMA
    return pl.pallas_call(
        functools.partial(level_one_kernel, rows, cols),
        out_shape=jax.ShapeDtypeStruct(rhs.shape, bf16),
        in_specs=[VMEM] * 5,
        out_specs=VMEM,
        scratch_shapes=[
            pltpu.VMEM((owners, leaves, size, half), bf16),
            pltpu.VMEM(blocks.shape, bf16),
            pltpu.VMEM(mask.shape, bf16),
            pltpu.VMEM((2, size, half), jnp.float32),
            pltpu.VMEM((2, cols // 2, size, share), bf16),
            pltpu.VMEM((cols, size, share), bf16),
            dma((2, owners)),
            dma((2,)),
            dma((rows, leaves)),
            dma((rows, leaves)),
            dma((2, cols // 2)),
            dma((cols,)),
        ],
        compiler_params=pltpu.CompilerParams(
            collective_id=1, has_side_effects=True, vmem_limit_bytes=48 * 2**20
        ),
        name="level_one",
    )(sol, blocks, mask, rhs, inverse)


def top_kernel(
    grids,
    rows,
    sol_ref,
    blocks_ref,
    rhs_ref,
    inverse_hbm,
    chain_hbm,
    out_ref,
    inverse_ref,
    chain_ref,
    terms,
    landed,
    load_sems,
    term_send,
    term_recv,
    out_send,
    out_recv,
):
    group = grids * rows
    me = lax.axis_index("grid") * rows + lax.axis_index("row")
    tops, size = blocks_ref.shape[0], blocks_ref.shape[1]
    depth = terms.shape[2]
    loads = (
        pltpu.make_async_copy(inverse_hbm, inverse_ref, load_sems.at[0]),
        pltpu.make_async_copy(chain_hbm, chain_ref, load_sems.at[1]),
    )
    for load in loads:
        load.start()
    greet(("grid", "row"), (grids, rows))
    turned = sol_ref[...].T

    def peer(step):
        return lax.rem(me + step, group)

    def term_copy(step, top, slot):
        target = peer(step)
        return pltpu.make_async_remote_copy(
            src_ref=terms.at[target, top],
            dst_ref=landed.at[slot, top],
            send_sem=term_send.at[target, top],
            recv_sem=term_recv.at[slot, top],
            device_id={"grid": target // rows, "row": lax.rem(target, rows)},
            device_id_type=MESH,
        )

    def out_copy(step, top, slot):
        target = peer(step)
        return pltpu.make_async_remote_copy(
            src_ref=out_ref.at[me, top],
            dst_ref=out_ref.at[slot, top],
            send_sem=out_send.at[target, top],
            recv_sem=out_recv.at[slot, top],
            device_id={"grid": target // rows, "row": lax.rem(target, rows)},
            device_id_type=MESH,
        )

    for top in range(tops):
        term = dot_t(turned, blocks_ref[top]).astype(terms.dtype)
        terms[:, top] = term.reshape(group, depth, size)

        @pl.loop(1, group)
        def _(step, top=top):
            term_copy(step, top, me).start()

    for load in loads:
        load.wait()
    for top in range(tops):

        @pl.loop(1, group)
        def _(step, top=top):
            term_copy(step, top, peer(step)).wait_recv()

        landed[me, top] = terms[me, top]
        update = landed[0, top].astype(jnp.float32)
        for other in range(1, group):
            update = update + landed[other, top].astype(jnp.float32)
        running = rhs_ref[top].astype(jnp.float32) - update
        for earlier in range(top):
            running = running - dot_t(
                out_ref[me, earlier], chain_ref[top * (top - 1) // 2 + earlier]
            )
        out_ref[me, top] = dot_t(running.astype(jnp.bfloat16), inverse_ref[top]).astype(
            jnp.bfloat16
        )

        @pl.loop(1, group)
        def _(step, top=top):
            out_copy(step, top, me).start()

    for top in range(tops):

        @pl.loop(1, group)
        def _(step, top=top):
            term_copy(step, top, me).wait_send()
            out_copy(step, top, me).wait_send()
            out_copy(step, top, peer(step)).wait_recv()


def top_stage(sol, blocks, top_rhs, inverse, chain):
    grids, rows = lax.axis_size("grid"), lax.axis_size("row")
    group = grids * rows
    tops, size, width = top_rhs.shape
    depth = width // group
    bf16 = jnp.bfloat16
    dma = pltpu.SemaphoreType.DMA
    offset = lax.axis_index(("grid", "row")) * depth
    rhs_turned = lax.dynamic_slice_in_dim(jnp.swapaxes(top_rhs, 1, 2), offset, depth, 1)
    stacked = pl.pallas_call(
        functools.partial(top_kernel, grids, rows),
        out_shape=jax.ShapeDtypeStruct((group, tops, depth, size), bf16),
        in_specs=[VMEM, VMEM, VMEM, ANY, ANY],
        out_specs=VMEM,
        scratch_shapes=[
            pltpu.VMEM(inverse.shape, bf16),
            pltpu.VMEM(chain.shape, bf16),
            pltpu.VMEM((group, tops, depth, size), bf16),
            pltpu.VMEM((group, tops, depth, size), bf16),
            dma((2,)),
            dma((group, tops)),
            dma((group, tops)),
            dma((group, tops)),
            dma((group, tops)),
        ],
        compiler_params=pltpu.CompilerParams(
            collective_id=2, has_side_effects=True, vmem_limit_bytes=32 * 2**20
        ),
        name="top",
    )(sol, blocks, rhs_turned, inverse, chain)
    return jnp.transpose(stacked, (1, 3, 0, 2)).reshape(tops, size, width)


def shards(
    rhs_in,
    rhs_target,
    leaf_inverse,
    level_one_blocks,
    level_one_pattern,
    level_one_rhs,
    level_one_inverse,
    top_blocks,
    top_rhs,
    top_inverse,
    top_chain,
):
    device_count = lax.axis_size(("grid", "row", "col"))
    rows_local, rhs_width = rhs_in.shape
    share_rows = rows_local // device_count
    destination = rhs_target // rows_local
    ordering = jnp.argsort(destination, stable=True)
    send_rows = rhs_in[ordering].reshape(device_count, share_rows, rhs_width)
    send_places = (rhs_target % rows_local)[ordering].reshape(device_count, share_rows)
    got_rows, got_places = (
        lax.all_to_all(send_rows, ("grid", "row", "col"), split_axis=0, concat_axis=0, tiled=True),
        lax.all_to_all(
            send_places, ("grid", "row", "col"), split_axis=0, concat_axis=0, tiled=True
        ),
    )
    placed = got_rows.reshape(rows_local, rhs_width)[jnp.argsort(got_places.reshape(rows_local))]
    leaf_count, block_size = (leaf_inverse.shape[0], leaf_inverse.shape[1])
    leaf_rhs = placed.reshape(leaf_count, block_size, rhs_width)
    leaf_solution = jnp.einsum(
        "lij,ljr->lir", leaf_inverse, leaf_rhs, preferred_element_type=jnp.float32
    ).astype(jnp.bfloat16)
    solution_one = level_one(
        leaf_solution,
        level_one_blocks[0, 0, 0],
        level_one_pattern[0, 0, 0],
        level_one_rhs[0, 0],
        level_one_inverse[0, 0],
    )
    top_solution = top_stage(solution_one, top_blocks[0, 0], top_rhs, top_inverse, top_chain)
    return (leaf_solution.reshape(rows_local, rhs_width), solution_one[None, None], top_solution)


def solution(mesh):
    in_specs = (
        P(("grid", "row", "col"), None),
        P(("grid", "row", "col")),
        P(("grid", "row", "col"), None, None),
        P("grid", "row", "col", None, None, None, None),
        P("grid", "row", "col", None, None),
        P("grid", "row", None, "col"),
        P("grid", "row", None, None),
        P("grid", "row", None, None, None),
        P(None, None, "col"),
        P(),
        P(),
    )
    out_specs = (
        P(("grid", "row", "col"), None),
        P("grid", "row", None, "col"),
        P(None, None, "col"),
    )
    return jax.shard_map(shards, mesh=mesh, in_specs=in_specs, out_specs=out_specs, check_vma=False)
```

time: 287 us -> 197 us (0.69)
  waiting for transfers between devices: 182 us -> 40 us
  Pallas kernels: 0 us -> 106 us
  matrix products: 29.1 us -> 2.92 us
  local copies, waits for them, and re-layouts: 36.2 us -> 22.9 us
  between operations: 13.9 us -> 0.83 us
    pallas_call x0 -> x2, Pallas kernels: none -> 106 us  [the longest x1 61.9 us: level_one(): pl.pallas_call(functools.partial(level_one_kernel, rows, cols), out_shape...]
    all_gather x2 -> x0, waiting for transfers between devices: 80.8 us -> none  [the longest x1 57.3 us: shards(): lax.all_gather(leaf_solution[None], 'row', axis=0, tiled=True)]
    reduce_scatter x2 -> x0, waiting for transfers between devices: 59.4 us -> none  [the longest x1 34.1 us: shards(): lax.psum_scatter(top_terms.astype(jnp.bfloat16), ('grid', 'row'), scatter...]
    dot_general x10 -> x0, matrix products: 24.9 us -> none  [the longest x1 10.1 us: shards(): jnp.einsum('nlij,nljr->ir', blocks, masked, preferred_element_type=jnp.fl...]
    all_gather x1 -> x0, local copies, waits for them, and re-layouts: 11.5 us -> none  [shards(): lax.all_gather(leaf_solution[None], 'row', axis=0, tiled=True)]
  transfers between devices with their start and end apart: 6 -> 2, of which waited for: 5 -> 1; matrix products, arithmetic and copies ran while one was open for 5% -> 6% of each run, Pallas kernels for 0% -> 0%
where the time goes in v1:
time: 197 us; the launch traced here: 195 us
  Pallas kernels  106 us (54%)
  waiting for transfers between devices  40 us (20%)
  local copies, waits for them, and re-layouts  22.9 us (12%)
  starting transfers between devices  12.1 us (6%)
  other arithmetic  10.3 us (5%)
  matrix products  2.92 us (1%)
    pallas_call x1, Pallas kernels, level_one(): pl.pallas_call(functools.partial(level_one_kernel, rows, cols), out_shape...  61.9 us
    pallas_call x1, Pallas kernels, top_stage(): pl.pallas_call(functools.partial(top_kernel, grids, rows), out_shape=jax....  44.2 us
    all_to_all x1, waiting for transfers between devices, shards(): lax.all_to_all(send_rows, ('grid', 'row', 'col'), split_axis=0, concat_ax...  40 us
    gather x1, local copies, waits for them, and re-layouts, shards(): got_rows.reshape(rows_local, rhs_width)  7.96 us
    all_to_all x1, starting transfers between devices, shards(): lax.all_to_all(send_places, ('grid', 'row', 'col'), split_axis=0, concat_...  6.22 us
    all_to_all x1, starting transfers between devices, shards(): lax.all_to_all(send_rows, ('grid', 'row', 'col'), split_axis=0, concat_ax...  5.89 us
    gather x1, local copies, waits for them, and re-layouts, shards(): send_rows = rhs_in[ordering].reshape(device_count, share_rows, rhs_width)  5.34 us
    gather x1, local copies, waits for them, and re-layouts, shards(): (rhs_target % rows_local)[ordering].reshape(device_count, share_rows)  4.52 us
  transfers between devices with their start and end apart: 2, of which 1 were waited for; matrix products, arithmetic and copies ran while one was open for 6% of the time, Pallas kernels for 0%

profile of v1, /device:TPU:17, one launch (start us, length us, event | category | flops | bytes accessed | tf_op | source)
XLA Modules:
  0.0 195.2 jit_solution(1806544469474464796)
XLA Ops:
  0.6 0.0 copy-start
  0.6 0.8 add_select_fusion
  1.5 4.4 %sort.34 = (s32[1024]{0:T(1024)}, s32[1024]{0:T(1024)S(1)}) sort(s32[1024]{0:T(1024)S(1)} %get-tuple-element.11, s32[1024]{0:T(1024)S(1)} %iota.8), dimensions={0}, to_apply=%region_0.1 | sort | flops 10240 | bytes 16384 | tf_op jit(solution)/shard_map/jit(argsort)/sort | solution.py:397
  5.9 4.5 %gather_fusion.1 = s32[1024]{0:T(1024)S(1)} fusion(s32[1024]{0:T(1024)S(1)} %get-tuple-element.10, s32[1024]{0:T(1024)S(1)} %fusion), kind=kCustom, calls=%fused_computation.1 | custom fusion | bytes 12288 | tf_op jit(solution)/shard_map/gather | solution.py:399
  10.4 0.7 all_to_all.10
  11.1 6.2 %all-to-all-start.1 = ((s32[32,1,32]{2,1,0:T(1,128)}), s32[32,1,32]{2,1,0:T(1,128)S(1)}, u32[]{:S(2)}, u32[]{:S(2)}) async-start(s32[32,1,32]{2,1,0:T(1,128)} %all_to_all.10), calls=%async_computation.1 | async-start | bytes 32768 | tf_op jit(solution)/shard_map/all_to_all | solution.py:402
  17.3 5.3 %gather_fusion = bf16[1024,1024]{1,0:T(8,128)(2,1)} fusion(bf16[1024,1024]{1,0:T(8,128)(2,1)S(1)} %copy-done, s32[1024]{0:T(1024)S(1)} %fusion), kind=kCustom, calls=%fused_computation | custom fusion | bytes 4198400 | tf_op jit(solution)/shard_map/gather | solution.py:398
  22.7 5.9 %all-to-all-start = ((bf16[32,32,1024]{2,1,0:T(8,128)(2,1)}), bf16[32,32,1024]{2,1,0:T(8,128)(2,1)}, u32[]{:S(2)}, u32[]{:S(2)}) async-start(bf16[32,32,1024]{2,1,0:T(8,128)(2,1)} %bitcast.26), calls=%async_computation | async-start | bytes 4194304 | tf_op jit(solution)/shard_map/all_to_all | solution.py:401
  28.6 1.3 constant_dynamic-slice_fusion
  29.8 0.2 copy.20
  30.0 0.1 copy.16
  30.1 0.5 broadcast.31
  30.7 0.7 reduce.3
  31.3 0.1 reshape.37
  31.4 4.4 %sort.35 = (s32[1024]{0:T(1024)}, s32[1024]{0:T(1024)S(1)}) sort(s32[1024]{0:T(1024)S(1)} %reshape.37, s32[1024]{0:T(1024)S(1)} %iota.9), dimensions={0}, to_apply=%region_1.2 | sort | flops 10240 | bytes 16384 | tf_op jit(solution)/shard_map/jit(argsort)/sort | solution.py:406
  35.8 40.0 %all-to-all-done = bf16[32,32,1024]{2,1,0:T(8,128)(2,1)} async-done(((bf16[32,32,1024]{2,1,0:T(8,128)(2,1)}), bf16[32,32,1024]{2,1,0:T(8,128)(2,1)}, u32[]{:S(2)}, u32[]{:S(2)}) %all-to-all-start) | async-done | bytes 2097184 | tf_op jit(solution)/shard_map/all_to_all | solution.py:401
  75.8 8.0 %gather_fusion.2 = bf16[1024,1024]{1,0:T(8,128)(2,1)} fusion(bf16[1024,1024]{1,0:T(8,128)(2,1)} %bitcast.1, s32[1024]{0:T(1024)S(1)} %fusion.1), kind=kCustom, calls=%fused_computation.2 | custom fusion | bytes 4198400 | tf_op jit(solution)/shard_map/gather | solution.py:406
  83.7 2.9 %convolution_convert_fusion = bf16[2,1024,512]{1,2,0:T(8,128)(2,1)S(1)} fusion(bf16[2,512,512]{2,1,0:T(8,128)(2,1)S(1)} %copy-done.7, bf16[2,512,1024]{2,1,0:T(8,128)(2,1)} %bitcast.29), kind=kOutput, calls=%fused_computation.3 | convolution fusion | flops 1074790400 | bytes 5242880 | tf_op jit(solution)/shard_map/lij,ljr->lir/dot_general | solution.py:409
  86.7 0.1 broadcast_in_dim.18.pattern_ref
  86.8 61.9 %level_one.1.sol_ref = bf16[512,256]{1,0:T(8,128)(2,1)S(1)} custom-call(bf16[2,512,1024]{2,1,0:T(8,128)(2,1)S(1)} %bitcast.20, bf16[4,2,512,512]{3,2,1,0:T(8,128)(2,1)} %bitcast.27, bf16[4,2,16,512]{3,2,1,0:T(8,128)(2,1)S(1)} %broadcast_in_dim.18.pattern_ref, bf16[512,256]{1,0:T(8,128)(2,1)S(1)} %bitcast.25, bf16[512,512]{1,0:T(8,128)(2,1)S(1)} %bitcast.23), custom_call_target="tpu_custom_call" | custom-call | tf_op jit(solution)/shard_map/level_one/pallas_call | solution.py:222
  148.8 44.2 %top.1 = bf16[8,4,32,512]{3,2,1,0:T(8,128)(2,1)S(1)} custom-call(bf16[512,256]{1,0:T(8,128)(2,1)S(1)} %level_one.1.sol_ref, bf16[4,512,512]{2,1,0:T(8,128)(2,1)S(1)} %bitcast.22, bf16[4,32,512]{2,1,0:T(8,128)(2,1)S(1)} %bitcast.24, bf16[4,512,512]{2,1,0:T(8,128)(2,1)S(1)} %copy-done.4, bf16[6,512,512]{2,1,0:T(8,128)(2,1)S(1)} %copy-done.1), custom_call_target="tpu_custom_call" | custom-call | tf_op jit(solution)/shard_map/top/pallas_call | solution.py:356
  193.1 0.1 copy.18
  193.2 1.3 copy.19
  194.5 0.7 copy.22
  (23 shorter events, 0.1 us)
Async XLA Ops:
  0.6 16.7 %copy-start = (bf16[1024,1024]{1,0:T(8,128)(2,1)S(1)}, bf16[1024,1024]{1,0:T(8,128)(2,1)}, u32[]{:S(2)}) copy-start(bf16[1024,1024]{1,0:T(8,128)(2,1)} %param.11) | copy-start | bytes 6291460
  11.1 11.6 %all-to-all-start.1 = ((s32[32,1,32]{2,1,0:T(1,128)}), s32[32,1,32]{2,1,0:T(1,128)S(1)}, u32[]{:S(2)}, u32[]{:S(2)}) async-start(s32[32,1,32]{2,1,0:T(1,128)} %all_to_all.10), calls=%async_computation.1 | async-start | bytes 32768 | tf_op jit(solution)/shard_map/all_to_all | solution.py:402
  22.7 7.3 %copy-start.8 = (s32[1,1,1,4,2]{3,4,2,1,0:T(2,128)S(1)}, s32[1,1,1,4,2]{3,4,2,1,0:T(2,128)}, u32[]{:S(2)}) copy-start(s32[1,1,1,4,2]{3,4,2,1,0:T(2,128)} %param.15) | copy-start | bytes 100
  22.7 53.1 %all-to-all-start = ((bf16[32,32,1024]{2,1,0:T(8,128)(2,1)}), bf16[32,32,1024]{2,1,0:T(8,128)(2,1)}, u32[]{:S(2)}, u32[]{:S(2)}) async-start(bf16[32,32,1024]{2,1,0:T(8,128)(2,1)} %bitcast.26), calls=%async_computation | async-start | bytes 4194304 | tf_op jit(solution)/shard_map/all_to_all | solution.py:401
  75.8 8.0 %copy-start.7 = (bf16[2,512,512]{2,1,0:T(8,128)(2,1)S(1)}, bf16[2,512,512]{2,1,0:T(8,128)(2,1)}, u32[]{:S(2)}) copy-start(bf16[2,512,512]{2,1,0:T(8,128)(2,1)} %param.13) | copy-start | bytes 3145732
  83.7 3.0 %copy-start.5 = (bf16[1,1,512,512]{3,2,1,0:T(8,128)(2,1)S(1)}, bf16[1,1,512,512]{3,2,1,0:T(8,128)(2,1)}, u32[]{:S(2)}) copy-start(bf16[1,1,512,512]{3,2,1,0:T(8,128)(2,1)} %param.17) | copy-start | bytes 1572868
  83.7 3.0 %copy-start.6 = (bf16[1,1,512,256]{3,2,1,0:T(8,128)(2,1)S(1)}, bf16[1,1,512,256]{3,2,1,0:T(8,128)(2,1)}, u32[]{:S(2)}) copy-start(bf16[1,1,512,256]{3,2,1,0:T(8,128)(2,1)} %param.16) | copy-start | bytes 786436
  86.7 62.1 %copy-start.2 = (bf16[2,1024,512]{1,2,0:T(8,128)(2,1)}, bf16[2,1024,512]{1,2,0:T(8,128)(2,1)S(1)}, u32[]{:S(2)}) copy-start(bf16[2,1024,512]{1,2,0:T(8,128)(2,1)S(1)} %convolution_convert_fusion) | copy-start | bytes 6291460
  86.8 62.0 %copy-start.1 = (bf16[6,512,512]{2,1,0:T(8,128)(2,1)S(1)}, bf16[6,512,512]{2,1,0:T(8,128)(2,1)}, u32[]{:S(2)}) copy-start(bf16[6,512,512]{2,1,0:T(8,128)(2,1)} %chain_hbm.1) | copy-start | bytes 9437188
  86.8 62.0 %copy-start.3 = (bf16[1,1,4,512,512]{4,3,2,1,0:T(8,128)(2,1)S(1)}, bf16[1,1,4,512,512]{4,3,2,1,0:T(8,128)(2,1)}, u32[]{:S(2)}) copy-start(bf16[1,1,4,512,512]{4,3,2,1,0:T(8,128)(2,1)} %param.18) | copy-start | bytes 6291460
  86.8 62.0 %copy-start.4 = (bf16[4,512,512]{2,1,0:T(8,128)(2,1)S(1)}, bf16[4,512,512]{2,1,0:T(8,128)(2,1)}, u32[]{:S(2)}) copy-start(bf16[4,512,512]{2,1,0:T(8,128)(2,1)} %inverse_hbm.1) | copy-start | bytes 6291460

commit v2 on v1

v2 whole, which is shorter than its diff:
```python
import functools

import jax
import jax.numpy as jnp
from jax import lax
from jax.experimental import pallas as pl
from jax.experimental.pallas import tpu as pltpu
from jax.sharding import PartitionSpec as P

MESH = pl.DeviceIdType.MESH
VMEM = pl.BlockSpec(memory_space=pltpu.VMEM)
ANY = pl.BlockSpec(memory_space=pl.ANY)


def greet(axes, sizes):
    barrier = pltpu.get_barrier_semaphore()
    total = 1
    for size in sizes:
        total *= size
    flat = 0
    for axis, size in zip(axes, sizes):
        flat = flat * size + lax.axis_index(axis)

    @pl.loop(1, total)
    def _(step):
        rest = lax.rem(flat + step, total)
        coords = {}
        for axis, size in reversed(list(zip(axes, sizes))):
            coords[axis] = lax.rem(rest, size)
            rest = rest // size
        pl.semaphore_signal(barrier, inc=1, device_id=coords, device_id_type=MESH)

    pl.semaphore_wait(barrier, total - 1)


def dot(a, b):
    return jnp.dot(a, b, preferred_element_type=jnp.float32)


def dot_t(a, b):
    return lax.dot_general(a, b, (((1,), (1,)), ((), ())), preferred_element_type=jnp.float32)


def lower_kernel(
    sizes,
    order,
    rhs_ref,
    slot_ref,
    place_ref,
    inverse_ref,
    blocks_hbm,
    pattern_ref,
    rhs_one_ref,
    inverse_one_ref,
    leaf_ref,
    one_ref,
    perm,
    fold,
    sorted_rows,
    got,
    got_places,
    own_blocks,
    other_blocks,
    other_pattern,
    solved,
    gathered,
    totals,
    pieces,
    landed,
    load_sems,
    block_sems,
    pattern_sems,
    place_send,
    place_recv,
    row_send,
    row_recv,
    gather_send,
    gather_recv,
    piece_send,
    piece_recv,
):
    grids, rows, cols = sizes
    devices = grids * rows * cols
    row = lax.axis_index("row")
    col = lax.axis_index("col")
    me = (lax.axis_index("grid") * rows + row) * cols + col
    side = lax.rem(row, 2)
    mate = row + 1 - 2 * side
    leaves, size, _ = inverse_ref.shape
    height = leaves * size
    chunk = leaf_ref.shape[1] // cols
    half = chunk // 2
    share = got.shape[2]
    group = 128 // share

    def row_at(offset):
        pair = lax.rem(row // 2 + offset // 2, rows // 2)
        return pair * 2 + lax.rem(side + offset % 2, 2)

    def device_of(flat):
        return {
            "grid": flat // (rows * cols),
            "row": lax.rem(flat // cols, rows),
            "col": lax.rem(flat, cols),
        }

    loads = [
        pltpu.make_async_copy(blocks_hbm.at[owner], own_blocks.at[owner], load_sems.at[owner])
        for owner in range(rows)
    ]
    for load in loads:
        load.start()

    greet(("grid", "row", "col"), sizes)

    def peer(step):
        return lax.rem(me + step, devices)

    def place_copy(step, slot):
        target = peer(step)
        return pltpu.make_async_remote_copy(
            src_ref=place_ref.at[target],
            dst_ref=got_places.at[slot],
            send_sem=place_send.at[target],
            recv_sem=place_recv.at[slot],
            device_id=device_of(target),
            device_id_type=MESH,
        )

    def row_copy(part, step, slot):
        target = peer(step)
        return pltpu.make_async_remote_copy(
            src_ref=sorted_rows.at[part, target],
            dst_ref=got.at[part, slot],
            send_sem=row_send.at[part, target],
            recv_sem=row_recv.at[part, slot],
            device_id=device_of(target),
            device_id_type=MESH,
        )

    def block_copy(owner):
        return pltpu.make_async_remote_copy(
            src_ref=blocks_hbm.at[owner],
            dst_ref=other_blocks.at[owner],
            send_sem=block_sems.at[0, owner],
            recv_sem=block_sems.at[1, owner],
            device_id={"row": mate},
            device_id_type=MESH,
        )

    def gather_copy(part, target, owner):
        return pltpu.make_async_remote_copy(
            src_ref=solved.at[part, lax.rem(target, 2)],
            dst_ref=gathered.at[part, owner],
            send_sem=gather_send.at[part, target],
            recv_sem=gather_recv.at[part, owner],
            device_id={"row": target},
            device_id_type=MESH,
        )

    def piece_copy(part, which, source, from_side):
        return pltpu.make_async_remote_copy(
            src_ref=pieces.at[part, which],
            dst_ref=landed.at[source, from_side],
            send_sem=piece_send.at[part, which],
            recv_sem=piece_recv.at[source, from_side],
            device_id={"row": mate if which else row, "col": part},
            device_id_type=MESH,
        )

    pattern_copy = pltpu.make_async_remote_copy(
        src_ref=pattern_ref,
        dst_ref=other_pattern,
        send_sem=pattern_sems.at[0],
        recv_sem=pattern_sems.at[1],
        device_id={"row": mate},
        device_id_type=MESH,
    )

    @pl.loop(1, devices)
    def _(step):
        place_copy(step, me).start()

    step_rows = 256
    for begin in range(0, height, step_rows):
        index = lax.broadcasted_iota(jnp.int32, (step_rows, height), 0) + begin
        perm[begin : begin + step_rows, :] = (
            jnp.where(index == slot_ref[...], 1.0, 0.0).astype(perm.dtype)
        )
    for part in order:
        moved = dot(perm[...], rhs_ref[:, part * chunk : (part + 1) * chunk]).astype(got.dtype)
        sorted_rows[part] = moved.reshape(devices, share, chunk)

        @pl.loop(1, devices)
        def _(step, part=part):
            row_copy(part, step, me).start()

        got[part, me] = sorted_rows[part, me]
    pattern_copy.start()
    for owner in range(rows):
        block_copy(owner).start()

    got_places[me] = place_ref[me]

    @pl.loop(1, devices)
    def _(step):
        place_copy(step, peer(step)).wait_recv()

    for block in range(height // 128):
        places = got_places[block * group]
        for other in range(1, group):
            places = places + got_places[block * group + other]
        index = lax.broadcasted_iota(jnp.int32, (height, 128), 0)
        perm[:, block * 128 : (block + 1) * 128] = jnp.where(index == places, 1.0, 0.0).astype(
            perm.dtype
        )
    for leaf in range(leaves):
        span = slice(leaf * size, (leaf + 1) * size)
        fold[span, :] = dot(inverse_ref[leaf], perm[span, :]).astype(fold.dtype)

    def masked(block, mask):
        tall = block.shape[0] // mask.shape[0]
        return (block.reshape(tall, *mask.shape) * mask[None]).reshape(block.shape)

    for load in loads:
        load.wait()

    @pl.loop(0, rows)
    def _(owner):
        for leaf in range(leaves):
            own_blocks[owner, leaf] = masked(own_blocks[owner, leaf], pattern_ref[owner, leaf])

    def solve(part):
        @pl.loop(1, devices)
        def _(step):
            row_copy(part, step, peer(step)).wait_recv()

        result = dot(fold[...], got[part].reshape(height, chunk)).astype(leaf_ref.dtype)
        leaf_ref[:, part * chunk : (part + 1) * chunk] = result
        for which in range(2):
            solved[part, which] = result[:, which * half : (which + 1) * half]
        for offset in range(rows - 1, 0, -1):
            gather_copy(part, row_at(offset), row).start()
        gathered[part, row] = solved[part, side]

    def add(part, owner):
        for which, blocks in enumerate((own_blocks, other_blocks)):
            term = dot(blocks[owner, 0], gathered[part, owner, :size])
            for leaf in range(1, leaves):
                term = term + dot(
                    blocks[owner, leaf], gathered[part, owner, leaf * size : (leaf + 1) * size]
                )
            totals[which] += term

    def couple(part):
        totals[...] = jnp.zeros_like(totals)

        @pl.loop(0, rows)
        def _(offset):
            owner = row_at(offset)

            @pl.when(offset > 0)
            def _():
                gather_copy(part, owner, owner).wait_recv()

            add(part, owner)

        pieces[part] = totals[...].astype(pieces.dtype)
        piece_copy(part, 1, col, side).start()

        @pl.when(col != part)
        def _():
            piece_copy(part, 0, col, side).start()

        @pl.when(col == part)
        def _():
            landed[col, side] = pieces[part, 0]

    for at, part in enumerate(order):
        solve(part)
        if at == 0:
            pattern_copy.wait()

            @pl.loop(0, rows)
            def _(owner):
                block_copy(owner).wait()
                for leaf in range(leaves):
                    other_blocks[owner, leaf] = masked(
                        other_blocks[owner, leaf], other_pattern[owner, leaf]
                    )
        else:
            couple(order[at - 1])
    couple(order[-1])

    for step in range(cols):
        source = lax.rem(col + step, cols)
        piece_copy(0, 1, source, 1 - side).wait_recv()
        if step:
            piece_copy(0, 0, source, side).wait_recv()
    update = []
    for which in range(2):
        total = landed[0, which].astype(jnp.float32)
        for source in range(1, cols):
            total = total + landed[source, which].astype(jnp.float32)
        update.append(total)
    resid = rhs_one_ref[...].astype(jnp.float32) - jnp.concatenate(update, axis=1)
    one_ref[...] = dot(inverse_one_ref[...], resid.astype(jnp.bfloat16)).astype(one_ref.dtype)

    for part in range(cols):
        piece_copy(part, 1, col, side).wait_send()

        @pl.when(col != part)
        def _(part=part):
            piece_copy(part, 0, col, side).wait_send()

        for offset in range(1, rows):
            gather_copy(part, row_at(offset), row).wait_send()

        @pl.loop(1, devices)
        def _(step, part=part):
            row_copy(part, step, me).wait_send()

    @pl.loop(1, devices)
    def _(step):
        place_copy(step, me).wait_send()


def lower_levels(rhs_in, target, leaf_inverse, blocks, pattern, rhs, inverse):
    sizes = tuple(lax.axis_size(axis) for axis in ("grid", "row", "col"))
    grids, rows, cols = sizes
    devices = grids * rows * cols
    height, width = rhs_in.shape
    share = height // devices
    owners, leaves, size, _ = blocks.shape
    chunk = width // cols
    half = chunk // 2
    bf16 = jnp.bfloat16
    order = sorted(range(cols), key=lambda part: -abs(2 * part - (cols - 1)))

    destination = target // height
    place = target % height
    index = jnp.arange(height, dtype=jnp.int32)
    same = (destination[:, None] == destination[None, :]) & (index[:, None] < index[None, :])
    slot = destination * share + jnp.sum(same.astype(jnp.int32), axis=0)
    picked = jnp.where(slot[None, :] == index[:, None], place[None, :], 0)
    sorted_places = jnp.sum(picked, axis=1).reshape(devices, 1, share)
    group = 128 // share
    me = lax.axis_index(("grid", "row", "col"))
    lane_group = jnp.arange(128, dtype=jnp.int32) // share
    place_rows = jnp.where(
        lane_group == me % group, jnp.tile(sorted_places, (1, 1, group)), 0
    )

    mask = jnp.broadcast_to(pattern.astype(bf16)[:, :, None, None], (owners, leaves, 16, size))
    dma = pltpu.SemaphoreType.DMA
    return pl.pallas_call(
        functools.partial(lower_kernel, sizes, order),
        out_shape=(
            jax.ShapeDtypeStruct((height, width), bf16),
            jax.ShapeDtypeStruct(rhs.shape, bf16),
        ),
        in_specs=[VMEM, VMEM, VMEM, VMEM, ANY, VMEM, VMEM, VMEM],
        out_specs=(VMEM, VMEM),
        scratch_shapes=[
            pltpu.VMEM((height, height), bf16),
            pltpu.VMEM((height, height), bf16),
            pltpu.VMEM((cols, devices, share, chunk), bf16),
            pltpu.VMEM((cols, devices, share, chunk), bf16),
            pltpu.VMEM((devices, 1, 128), jnp.int32),
            pltpu.VMEM(blocks.shape, bf16),
            pltpu.VMEM(blocks.shape, bf16),
            pltpu.VMEM(mask.shape, bf16),
            pltpu.VMEM((cols, 2, height, half), bf16),
            pltpu.VMEM((cols, rows, height, half), bf16),
            pltpu.VMEM((2, size, half), jnp.float32),
            pltpu.VMEM((cols, 2, size, half), bf16),
            pltpu.VMEM((cols, 2, size, half), bf16),
            dma((rows,)),
            dma((2, rows)),
            dma((2,)),
            dma((devices,)),
            dma((devices,)),
            dma((cols, devices)),
            dma((cols, devices)),
            dma((cols, rows)),
            dma((cols, rows)),
            dma((cols, 2)),
            dma((cols, 2)),
        ],
        compiler_params=pltpu.CompilerParams(
            collective_id=1, has_side_effects=True, vmem_limit_bytes=56 * 2**20
        ),
        name="lower",
    )(rhs_in, slot[None, :], place_rows, leaf_inverse, blocks, mask, rhs, inverse)


def top_kernel(
    grids,
    rows,
    sol_ref,
    blocks_ref,
    rhs_ref,
    inverse_hbm,
    chain_hbm,
    out_ref,
    inverse_ref,
    chain_ref,
    terms,
    landed,
    load_sems,
    term_send,
    term_recv,
    out_send,
    out_recv,
):
    group = grids * rows
    me = lax.axis_index("grid") * rows + lax.axis_index("row")
    tops, size = blocks_ref.shape[0], blocks_ref.shape[1]
    depth = terms.shape[2]
    loads = (
        pltpu.make_async_copy(inverse_hbm, inverse_ref, load_sems.at[0]),
        pltpu.make_async_copy(chain_hbm, chain_ref, load_sems.at[1]),
    )
    for load in loads:
        load.start()
    greet(("grid", "row"), (grids, rows))
    turned = sol_ref[...].T

    def peer(step):
        return lax.rem(me + step, group)

    def term_copy(step, top, slot):
        target = peer(step)
        return pltpu.make_async_remote_copy(
            src_ref=terms.at[target, top],
            dst_ref=landed.at[slot, top],
            send_sem=term_send.at[target, top],
            recv_sem=term_recv.at[slot, top],
            device_id={"grid": target // rows, "row": lax.rem(target, rows)},
            device_id_type=MESH,
        )

    def out_copy(step, top, slot):
        target = peer(step)
        return pltpu.make_async_remote_copy(
            src_ref=out_ref.at[me, top],
            dst_ref=out_ref.at[slot, top],
            send_sem=out_send.at[target, top],
            recv_sem=out_recv.at[slot, top],
            device_id={"grid": target // rows, "row": lax.rem(target, rows)},
            device_id_type=MESH,
        )

    for top in range(tops):
        term = dot_t(turned, blocks_ref[top]).astype(terms.dtype)
        terms[:, top] = term.reshape(group, depth, size)

        @pl.loop(1, group)
        def _(step, top=top):
            term_copy(step, top, me).start()

    for load in loads:
        load.wait()
    for top in range(tops):

        @pl.loop(1, group)
        def _(step, top=top):
            term_copy(step, top, peer(step)).wait_recv()

        landed[me, top] = terms[me, top]
        update = landed[0, top].astype(jnp.float32)
        for other in range(1, group):
            update = update + landed[other, top].astype(jnp.float32)
        running = rhs_ref[top].astype(jnp.float32) - update
        for earlier in range(top):
            running = running - dot_t(
                out_ref[me, earlier], chain_ref[top * (top - 1) // 2 + earlier]
            )
        out_ref[me, top] = dot_t(running.astype(jnp.bfloat16), inverse_ref[top]).astype(
            jnp.bfloat16
        )

        @pl.loop(1, group)
        def _(step, top=top):
            out_copy(step, top, me).start()

    for top in range(tops):

        @pl.loop(1, group)
        def _(step, top=top):
            term_copy(step, top, me).wait_send()
            out_copy(step, top, me).wait_send()
            out_copy(step, top, peer(step)).wait_recv()


def top_stage(sol, blocks, top_rhs, inverse, chain):
    grids, rows = lax.axis_size("grid"), lax.axis_size("row")
    group = grids * rows
    tops, size, width = top_rhs.shape
    depth = width // group
    bf16 = jnp.bfloat16
    dma = pltpu.SemaphoreType.DMA
    offset = lax.axis_index(("grid", "row")) * depth
    rhs_turned = lax.dynamic_slice_in_dim(jnp.swapaxes(top_rhs, 1, 2), offset, depth, 1)
    stacked = pl.pallas_call(
        functools.partial(top_kernel, grids, rows),
        out_shape=jax.ShapeDtypeStruct((group, tops, depth, size), bf16),
        in_specs=[VMEM, VMEM, VMEM, ANY, ANY],
        out_specs=VMEM,
        scratch_shapes=[
            pltpu.VMEM(inverse.shape, bf16),
            pltpu.VMEM(chain.shape, bf16),
            pltpu.VMEM((group, tops, depth, size), bf16),
            pltpu.VMEM((group, tops, depth, size), bf16),
            dma((2,)),
            dma((group, tops)),
            dma((group, tops)),
            dma((group, tops)),
            dma((group, tops)),
        ],
        compiler_params=pltpu.CompilerParams(
            collective_id=2, has_side_effects=True, vmem_limit_bytes=32 * 2**20
        ),
        name="top",
    )(sol, blocks, rhs_turned, inverse, chain)
    return jnp.transpose(stacked, (1, 3, 0, 2)).reshape(tops, size, width)


def shards(
    rhs_in,
    rhs_target,
    leaf_inverse,
    level_one_blocks,
    level_one_pattern,
    level_one_rhs,
    level_one_inverse,
    top_blocks,
    top_rhs,
    top_inverse,
    top_chain,
):
    leaf_solution, solution_one = lower_levels(
        rhs_in,
        rhs_target,
        leaf_inverse,
        level_one_blocks[0, 0, 0],
        level_one_pattern[0, 0, 0],
        level_one_rhs[0, 0],
        level_one_inverse[0, 0],
    )
    top_solution = top_stage(solution_one, top_blocks[0, 0], top_rhs, top_inverse, top_chain)
    return (leaf_solution, solution_one[None, None], top_solution)


def solution(mesh):
    in_specs = (
        P(("grid", "row", "col"), None),
        P(("grid", "row", "col")),
        P(("grid", "row", "col"), None, None),
        P("grid", "row", "col", None, None, None, None),
        P("grid", "row", "col", None, None),
        P("grid", "row", None, "col"),
        P("grid", "row", None, None),
        P("grid", "row", None, None, None),
        P(None, None, "col"),
        P(),
        P(),
    )
    out_specs = (
        P(("grid", "row", "col"), None),
        P("grid", "row", None, "col"),
        P(None, None, "col"),
    )
    return jax.shard_map(shards, mesh=mesh, in_specs=in_specs, out_specs=out_specs, check_vma=False)
```

time: 197 us -> 149 us (0.76)
  waiting for transfers between devices: 40 us -> 0 us
  Pallas kernels: 106 us -> 131 us
  starting transfers between devices: 12.1 us -> 0 us
  local copies, waits for them, and re-layouts: 22.9 us -> 12.9 us
  other arithmetic: 10.3 us -> 3.71 us
  matrix products: 2.92 us -> 0 us
    pallas_call x1, Pallas kernels: 61.9 us -> 104 us  [lower_levels(): pl.pallas_call(functools.partial(lower_kernel, sizes, order), out_shape=(...]
    all_to_all x2 -> x0, waiting for transfers between devices: 40 us -> none  [the longest x1 40 us: shards(): lax.all_to_all(send_rows, ('grid', 'row', 'col'), split_axis=0, concat_ax...]
    gather x3 -> x0, local copies, waits for them, and re-layouts: 17.8 us -> none  [the longest x1 7.96 us: shards(): got_rows.reshape(rows_local, rhs_width)]
    pallas_call x1, Pallas kernels: 44.2 us -> 27.4 us  [top_stage(): pl.pallas_call(functools.partial(top_kernel, grids, rows), out_shape=jax....]
    all_to_all x2 -> x0, starting transfers between devices: 12.1 us -> none  [the longest x1 6.22 us: shards(): lax.all_to_all(send_places, ('grid', 'row', 'col'), split_axis=0, concat_...]
    sort x2 -> x0, other arithmetic: 8.74 us -> none  [the longest x1 4.37 us: shards(): jnp.argsort(got_places.reshape(rows_local))]
    unnamed x21 -> x18, local copies, waits for them, and re-layouts: 2.25 us -> 10.8 us
    dot_general x1 -> x0, matrix products: 2.92 us -> none  [shards(): jnp.einsum('lij,ljr->lir', leaf_inverse, leaf_rhs, preferred_element_type...]
  transfers between devices with their start and end apart: 2 -> 0, of which waited for: 1 -> 0; matrix products, arithmetic and copies ran while one was open for 6% -> 0% of each run, Pallas kernels for 0% -> 0%
where the time goes in v2:
time: 149 us; the launch traced here: 148 us
  Pallas kernels  131 us (88%)
  local copies, waits for them, and re-layouts  12.9 us (9%)
  other arithmetic  3.71 us (2%)
    pallas_call x1, Pallas kernels, lower_levels(): pl.pallas_call(functools.partial(lower_kernel, sizes, order), out_shape=(...  104 us
    pallas_call x1, Pallas kernels, top_stage(): pl.pallas_call(functools.partial(top_kernel, grids, rows), out_shape=jax....  27.4 us
    unnamed x18, local copies, waits for them, and re-layouts  10.8 us

profile of v2, /device:TPU:17, one launch (start us, length us, event | category | flops | bytes accessed | tf_op | source)
XLA Modules:
  0.0 148.4 jit_solution(10679274208330816879)
XLA Ops:
  0.6 0.0 copy-start
  0.6 0.8 add_select_fusion.1
  1.4 0.4 convert_reduce_fusion
  1.8 0.7 add_select_fusion
  2.6 0.5 select_reduce_fusion
  3.1 0.1 tile.10
  3.1 0.1 tile.12
  3.3 0.6 broadcast_select_fusion.place_ref
  3.9 0.7 convert_bitcast_fusion
  4.6 0.1 copy.20
  4.7 0.7 broadcast_in_dim.44.pattern_ref
  5.4 103.7 %lower.1 = (bf16[1024,1024]{1,0:T(8,128)(2,1)}, bf16[512,256]{1,0:T(8,128)(2,1)}) custom-call(bf16[1024,1024]{1,0:T(8,128)(2,1)} %rhs_ref.1, s32[1,1024]{1,0:T(1,128)} %bitcast.19, s32[32,1,128]{2,1,0:T(1,128)} %broadcast_select_fusion.place_ref, bf16[2,512,512]{2,1,0:T(8,128)(2,1)} %inverse_ref.1, bf16[4,2,512,512]{3,2,1,0:T(8,128)(2,1)} %bitcast.15, ...), custom_call_target="tpu_custom_call" | custom-call | tf_op jit(solution)/shard_map/lower/pallas_call | solution.py:356
  109.1 0.0 copy-done
  109.2 1.0 constant_dynamic-slice_fusion
  110.2 1.2 copy.24
  111.4 0.0 copy-start.1
  111.4 1.9 %copy-done.1 = bf16[6,512,512]{2,1,0:T(8,128)(2,1)S(1)} copy-done((bf16[6,512,512]{2,1,0:T(8,128)(2,1)S(1)}, bf16[6,512,512]{2,1,0:T(8,128)(2,1)}, u32[]{:S(2)}) %copy-start.1) | copy-done | bytes 3145752
  113.3 1.6 %copy-done.3 = bf16[4,512,512]{2,1,0:T(8,128)(2,1)S(1)} copy-done((bf16[4,512,512]{2,1,0:T(8,128)(2,1)S(1)}, bf16[4,512,512]{2,1,0:T(8,128)(2,1)}, u32[]{:S(2)}) %copy-start.3) | copy-done | bytes 2097176
  114.9 0.9 copy-done.4
  115.8 27.4 %top.1 = bf16[8,4,32,512]{3,2,1,0:T(8,128)(2,1)S(1)} custom-call(bf16[512,256]{1,0:T(8,128)(2,1)S(1)} %copy-done.4, bf16[4,512,512]{2,1,0:T(8,128)(2,1)S(1)} %bitcast.12, bf16[4,32,512]{2,1,0:T(8,128)(2,1)S(1)} %bitcast.14, bf16[4,512,512]{2,1,0:T(8,128)(2,1)S(1)} %copy-done.3, bf16[6,512,512]{2,1,0:T(8,128)(2,1)S(1)} %copy-done.1), custom_call_target="tpu_custom_call" | custom-call | tf_op jit(solution)/shard_map/top/pallas_call | solution.py:505
  143.2 0.1 copy.22
  143.3 1.3 copy.23
  144.6 3.1 %copy.27 = bf16[1024,1024]{1,0:T(8,128)(2,1)} copy(bf16[1024,1024]{1,0:T(8,128)(2,1)} %get-tuple-element.18) | data formatting | bytes 4194304
  147.7 0.7 copy.28
  (10 shorter events, 0.0 us)
Async XLA Ops:
  0.6 108.5 %copy-start = (bf16[4,512,256]{2,1,0:T(8,128)(2,1)S(1)}, bf16[4,512,256]{2,1,0:T(8,128)(2,1)}, u32[]{:S(2)}) copy-start(bf16[4,512,256]{2,1,0:T(8,128)(2,1)} %param.19) | copy-start | bytes 3145732
  2.5 2.9 %copy-start.6 = (s32[1024]{0:T(1024)}, s32[1024]{0:T(1024)S(1)}, u32[]{:S(2)}) copy-start(s32[1024]{0:T(1024)S(1)} %get-tuple-element.14) | copy-start | bytes 12292
  5.4 105.9 %copy-start.2 = (bf16[1,1,4,512,512]{4,3,2,1,0:T(8,128)(2,1)S(1)}, bf16[1,1,4,512,512]{4,3,2,1,0:T(8,128)(2,1)}, u32[]{:S(2)}) copy-start(bf16[1,1,4,512,512]{4,3,2,1,0:T(8,128)(2,1)} %param.18) | copy-start | bytes 6291460
  111.4 1.9 %copy-start.1 = (bf16[6,512,512]{2,1,0:T(8,128)(2,1)S(1)}, bf16[6,512,512]{2,1,0:T(8,128)(2,1)}, u32[]{:S(2)}) copy-start(bf16[6,512,512]{2,1,0:T(8,128)(2,1)} %chain_hbm.1) | copy-start | bytes 9437188
  113.3 1.6 %copy-start.3 = (bf16[4,512,512]{2,1,0:T(8,128)(2,1)S(1)}, bf16[4,512,512]{2,1,0:T(8,128)(2,1)}, u32[]{:S(2)}) copy-start(bf16[4,512,512]{2,1,0:T(8,128)(2,1)} %inverse_hbm.1) | copy-start | bytes 6291460
  114.9 0.9 copy-start.4
  143.2 4.5 %copy-start.5 = (bf16[512,256]{1,0:T(8,128)(2,1)S(1)}, bf16[512,256]{1,0:T(8,128)(2,1)}, u32[]{:S(2)}) copy-start(bf16[512,256]{1,0:T(8,128)(2,1)} %get-tuple-element.6.sol_ref) | copy-start | bytes 786436

commit v3 on v2

--- a/solution.py
+++ b/solution.py
@@ -30,7 +30,7 @@
             rest = rest // size
         pl.semaphore_signal(barrier, inc=1, device_id=coords, device_id_type=MESH)
 
-    pl.semaphore_wait(barrier, total - 1)
+    return lambda: pl.semaphore_wait(barrier, total - 1)
 
 
 def dot(a, b):
@@ -52,8 +52,13 @@
     pattern_ref,
     rhs_one_ref,
     inverse_one_ref,
+    top_blocks_hbm,
+    top_rhs_hbm,
+    top_inverse_hbm,
+    chain_hbm,
     leaf_ref,
     one_ref,
+    top_ref,
     perm,
     fold,
     sorted_rows,
@@ -67,7 +72,17 @@
     totals,
     pieces,
     landed,
+    top_blocks,
+    top_rhs,
+    top_inverse,
+    chain,
+    rhs_turned,
+    terms,
+    mate_terms,
+    summed,
+    sums,
     load_sems,
+    top_load_sems,
     block_sems,
     pattern_sems,
     place_send,
@@ -78,6 +93,14 @@
     gather_recv,
     piece_send,
     piece_recv,
+    mate_send,
+    mate_recv,
+    sum_send,
+    sum_recv,
+    out_send,
+    out_recv,
+    on_send,
+    on_recv,
 ):
     grids, rows, cols = sizes
     devices = grids * rows * cols
@@ -108,10 +131,22 @@
         pltpu.make_async_copy(blocks_hbm.at[owner], own_blocks.at[owner], load_sems.at[owner])
         for owner in range(rows)
     ]
+    met = greet(("grid", "row", "col"), sizes)
     for load in loads:
         load.start()
-
-    greet(("grid", "row", "col"), sizes)
+    top_loads = [
+        pltpu.make_async_copy(source, into, top_load_sems.at[at])
+        for at, (source, into) in enumerate(
+            (
+                (top_rhs_hbm, top_rhs),
+                (top_blocks_hbm, top_blocks),
+                (top_inverse_hbm, top_inverse),
+                (chain_hbm, chain),
+            )
+        )
+    ]
+    for load in top_loads:
+        load.start()
 
     def peer(step):
         return lax.rem(me + step, devices)
@@ -177,24 +212,30 @@
         device_id_type=MESH,
     )
 
-    @pl.loop(1, devices)
-    def _(step):
-        place_copy(step, me).start()
-
     step_rows = 256
     for begin in range(0, height, step_rows):
         index = lax.broadcasted_iota(jnp.int32, (step_rows, height), 0) + begin
         perm[begin : begin + step_rows, :] = (
             jnp.where(index == slot_ref[...], 1.0, 0.0).astype(perm.dtype)
         )
-    for part in order:
+
+    def send_rows(part):
+        @pl.loop(1, devices)
+        def _(step):
+            row_copy(part, step, me).start()
+
+    for at, part in enumerate(order):
         moved = dot(perm[...], rhs_ref[:, part * chunk : (part + 1) * chunk]).astype(got.dtype)
         sorted_rows[part] = moved.reshape(devices, share, chunk)
-
-        @pl.loop(1, devices)
-        def _(step, part=part):
-            row_copy(part, step, me).start()
-
+        if at == 0:
+            met()
+
+            @pl.loop(1, devices)
+            def _(step):
+                place_copy(step, me).start()
+
+        if at < 2:
+            send_rows(part)
         got[part, me] = sorted_rows[part, me]
     pattern_copy.start()
     for owner in range(rows):
@@ -222,8 +263,14 @@
         tall = block.shape[0] // mask.shape[0]
         return (block.reshape(tall, *mask.shape) * mask[None]).reshape(block.shape)
 
-    for load in loads:
+    for load in loads + top_loads:
         load.wait()
+
+    tops = top_blocks.shape[0]
+    pairs = grids * rows // 2
+    depth = terms.shape[3]
+    for top in range(tops):
+        rhs_turned[top] = top_rhs[top].T.reshape(2 * pairs, depth, size)
 
     @pl.loop(0, rows)
     def _(owner):
@@ -278,6 +325,8 @@
 
     for at, part in enumerate(order):
         solve(part)
+        if at + 2 < cols:
+            send_rows(order[at + 2])
         if at == 0:
             pattern_copy.wait()
 
@@ -304,7 +353,108 @@
             total = total + landed[source, which].astype(jnp.float32)
         update.append(total)
     resid = rhs_one_ref[...].astype(jnp.float32) - jnp.concatenate(update, axis=1)
-    one_ref[...] = dot(inverse_one_ref[...], resid.astype(jnp.bfloat16)).astype(one_ref.dtype)
+    solution_one = dot(inverse_one_ref[...], resid.astype(jnp.bfloat16)).astype(one_ref.dtype)
+    one_ref[...] = solution_one
+
+    pair = (lax.axis_index("grid") * rows + row) // 2
+    here = 2 * pair + side
+
+    def pair_at(step):
+        return lax.rem(pair + step, pairs)
+
+    def across(target):
+        return {
+            "grid": target // (rows // 2),
+            "row": lax.rem(target, rows // 2) * 2 + side,
+        }
+
+    def mate_copy(top):
+        return pltpu.make_async_remote_copy(
+            src_ref=terms.at[top, 1 - side],
+            dst_ref=mate_terms.at[top],
+            send_sem=mate_send.at[top],
+            recv_sem=mate_recv.at[top],
+            device_id={"row": mate},
+            device_id_type=MESH,
+        )
+
+    def sum_copy(top, target, source):
+        return pltpu.make_async_remote_copy(
+            src_ref=summed.at[top, target],
+            dst_ref=sums.at[top, source],
+            send_sem=sum_send.at[top, target],
+            recv_sem=sum_recv.at[top, source],
+            device_id=across(target),
+            device_id_type=MESH,
+        )
+
+    def out_copy(top, target, source):
+        return pltpu.make_async_remote_copy(
+            src_ref=top_ref.at[here, top],
+            dst_ref=top_ref.at[2 * source + side, top],
+            send_sem=out_send.at[top, target],
+            recv_sem=out_recv.at[top, source],
+            device_id=across(target),
+            device_id_type=MESH,
+        )
+
+    def on_copy(top, source, from_side):
+        return pltpu.make_async_remote_copy(
+            src_ref=top_ref.at[2 * source + side, top],
+            dst_ref=top_ref.at[2 * source + from_side, top],
+            send_sem=on_send.at[top, source],
+            recv_sem=on_recv.at[top, source],
+            device_id={"row": mate},
+            device_id_type=MESH,
+        )
+
+    turned = solution_one.T
+    for top in range(tops):
+        term = dot_t(turned, top_blocks[top])
+        for target in range(2 * pairs):
+            terms[top, target % 2, target // 2] = term[
+                target * depth : (target + 1) * depth
+            ].astype(terms.dtype)
+        mate_copy(top).start()
+    for top in range(tops):
+        mate_copy(top).wait_recv()
+        summed[top] = (
+            terms[top, side].astype(jnp.float32) + mate_terms[top].astype(jnp.float32)
+        ).astype(summed.dtype)
+        for step in range(1, pairs):
+            sum_copy(top, pair_at(step), pair).start()
+    for top in range(tops):
+        sums[top, pair] = summed[top, pair]
+        for step in range(1, pairs):
+            sum_copy(top, pair_at(step), pair_at(step)).wait_recv()
+        update = sums[top, 0].astype(jnp.float32)
+        for other in range(1, pairs):
+            update = update + sums[top, other].astype(jnp.float32)
+        running = rhs_turned[top, here].astype(jnp.float32) - update
+        for earlier in range(top):
+            running = running - dot_t(
+                top_ref[here, earlier], chain[top * (top - 1) // 2 + earlier]
+            )
+        top_ref[here, top] = dot_t(running.astype(jnp.bfloat16), top_inverse[top]).astype(
+            top_ref.dtype
+        )
+        for step in range(1, pairs):
+            out_copy(top, pair_at(step), pair).start()
+        on_copy(top, pair, side).start()
+    for top in range(tops):
+        for step in range(1, pairs):
+            source = pair_at(step)
+            out_copy(top, source, source).wait_recv()
+            on_copy(top, source, side).start()
+    for top in range(tops):
+        for step in range(pairs):
+            on_copy(top, pair_at(step), 1 - side).wait_recv()
+        for step in range(pairs):
+            on_copy(top, pair_at(step), side).wait_send()
+            if step:
+                out_copy(top, pair_at(step), pair).wait_send()
+                sum_copy(top, pair_at(step), pair).wait_send()
+        mate_copy(top).wait_send()
 
     for part in range(cols):
         piece_copy(part, 1, col, side).wait_send()
@@ -325,7 +475,7 @@
         place_copy(step, me).wait_send()
 
 
-def lower_levels(rhs_in, target, leaf_inverse, blocks, pattern, rhs, inverse):
+def all_levels(rhs_in, target, leaf_inverse, blocks, pattern, rhs, inverse, *top_arrays):
     sizes = tuple(lax.axis_size(axis) for axis in ("grid", "row", "col"))
     grids, rows, cols = sizes
     devices = grids * rows * cols
@@ -353,14 +503,18 @@
 
     mask = jnp.broadcast_to(pattern.astype(bf16)[:, :, None, None], (owners, leaves, 16, size))
     dma = pltpu.SemaphoreType.DMA
-    return pl.pallas_call(
+    tops, _, top_width = top_arrays[1].shape
+    pairs = grids * rows // 2
+    depth = top_width // (2 * pairs)
+    leaf, one, stacked = pl.pallas_call(
         functools.partial(lower_kernel, sizes, order),
         out_shape=(
             jax.ShapeDtypeStruct((height, width), bf16),
             jax.ShapeDtypeStruct(rhs.shape, bf16),
+            jax.ShapeDtypeStruct((2 * pairs, tops, depth, size), bf16),
         ),
-        in_specs=[VMEM, VMEM, VMEM, VMEM, ANY, VMEM, VMEM, VMEM],
-        out_specs=(VMEM, VMEM),
+        in_specs=[VMEM, VMEM, VMEM, VMEM, ANY, VMEM, VMEM, VMEM, ANY, ANY, ANY, ANY],
+        out_specs=(VMEM, VMEM, VMEM),
         scratch_shapes=[
             pltpu.VMEM((height, height), bf16),
             pltpu.VMEM((height, height), bf16),
@@ -375,7 +529,14 @@
             pltpu.VMEM((2, size, half), jnp.float32),
             pltpu.VMEM((cols, 2, size, half), bf16),
             pltpu.VMEM((cols, 2, size, half), bf16),
+            *(pltpu.VMEM(array.shape, bf16) for array in top_arrays),
+            pltpu.VMEM((tops, 2 * pairs, depth, size), bf16),
+            pltpu.VMEM((tops, 2, pairs, depth, size), bf16),
+            pltpu.VMEM((tops, pairs, depth, size), bf16),
+            pltpu.VMEM((tops, pairs, depth, size), bf16),
+            pltpu.VMEM((tops, pairs, depth, size), bf16),
             dma((rows,)),
+            dma((len(top_arrays),)),
             dma((2, rows)),
             dma((2,)),
             dma((devices,)),
@@ -386,144 +547,17 @@
             dma((cols, rows)),
             dma((cols, 2)),
             dma((cols, 2)),
+            dma((tops,)),
+            dma((tops,)),
+            *(dma((tops, pairs)) for _ in range(6)),
         ],
         compiler_params=pltpu.CompilerParams(
-            collective_id=1, has_side_effects=True, vmem_limit_bytes=56 * 2**20
+            collective_id=1, has_side_effects=True, vmem_limit_bytes=60 * 2**20
         ),
         name="lower",
-    )(rhs_in, slot[None, :], place_rows, leaf_inverse, blocks, mask, rhs, inverse)
-
-
-def top_kernel(
-    grids,
-    rows,
-    sol_ref,
-    blocks_ref,
-    rhs_ref,
-    inverse_hbm,
-    chain_hbm,
-    out_ref,
-    inverse_ref,
-    chain_ref,
-    terms,
-    landed,
-    load_sems,
-    term_send,
-    term_recv,
-    out_send,
-    out_recv,
-):
-    group = grids * rows
-    me = lax.axis_index("grid") * rows + lax.axis_index("row")
-    tops, size = blocks_ref.shape[0], blocks_ref.shape[1]
-    depth = terms.shape[2]
-    loads = (
-        pltpu.make_async_copy(inverse_hbm, inverse_ref, load_sems.at[0]),
-        pltpu.make_async_copy(chain_hbm, chain_ref, load_sems.at[1]),
-    )
-    for load in loads:
-        load.start()
-    greet(("grid", "row"), (grids, rows))
-    turned = sol_ref[...].T
-
-    def peer(step):
-        return lax.rem(me + step, group)
-
-    def term_copy(step, top, slot):
-        target = peer(step)
-        return pltpu.make_async_remote_copy(
-            src_ref=terms.at[target, top],
-            dst_ref=landed.at[slot, top],
-            send_sem=term_send.at[target, top],
-            recv_sem=term_recv.at[slot, top],
-            device_id={"grid": target // rows, "row": lax.rem(target, rows)},
-            device_id_type=MESH,
-        )
-
-    def out_copy(step, top, slot):
-        target = peer(step)
-        return pltpu.make_async_remote_copy(
-            src_ref=out_ref.at[me, top],
-            dst_ref=out_ref.at[slot, top],
-            send_sem=out_send.at[target, top],
-            recv_sem=out_recv.at[slot, top],
-            device_id={"grid": target // rows, "row": lax.rem(target, rows)},
-            device_id_type=MESH,
-        )
-
-    for top in range(tops):
-        term = dot_t(turned, blocks_ref[top]).astype(terms.dtype)
-        terms[:, top] = term.reshape(group, depth, size)
-
-        @pl.loop(1, group)
-        def _(step, top=top):
-            term_copy(step, top, me).start()
-
-    for load in loads:
-        load.wait()
-    for top in range(tops):
-
-        @pl.loop(1, group)
-        def _(step, top=top):
-            term_copy(step, top, peer(step)).wait_recv()
-
-        landed[me, top] = terms[me, top]
-        update = landed[0, top].astype(jnp.float32)
-        for other in range(1, group):
-            update = update + landed[other, top].astype(jnp.float32)
-        running = rhs_ref[top].astype(jnp.float32) - update
-        for earlier in range(top):
-            running = running - dot_t(
-                out_ref[me, earlier], chain_ref[top * (top - 1) // 2 + earlier]
-            )
-        out_ref[me, top] = dot_t(running.astype(jnp.bfloat16), inverse_ref[top]).astype(
-            jnp.bfloat16
-        )
-
-        @pl.loop(1, group)
-        def _(step, top=top):
-            out_copy(step, top, me).start()
-
-    for top in range(tops):
-
-        @pl.loop(1, group)
-        def _(step, top=top):
-            term_copy(step, top, me).wait_send()
-            out_copy(step, top, me).wait_send()
-            out_copy(step, top, peer(step)).wait_recv()
-
-
-def top_stage(sol, blocks, top_rhs, inverse, chain):
-    grids, rows = lax.axis_size("grid"), lax.axis_size("row")
-    group = grids * rows
-    tops, size, width = top_rhs.shape
-    depth = width // group
-    bf16 = jnp.bfloat16
-    dma = pltpu.SemaphoreType.DMA
-    offset = lax.axis_index(("grid", "row")) * depth
-    rhs_turned = lax.dynamic_slice_in_dim(jnp.swapaxes(top_rhs, 1, 2), offset, depth, 1)
-    stacked = pl.pallas_call(
-        functools.partial(top_kernel, grids, rows),
-        out_shape=jax.ShapeDtypeStruct((group, tops, depth, size), bf16),
-        in_specs=[VMEM, VMEM, VMEM, ANY, ANY],
-        out_specs=VMEM,
-        scratch_shapes=[
-            pltpu.VMEM(inverse.shape, bf16),
-            pltpu.VMEM(chain.shape, bf16),
-            pltpu.VMEM((group, tops, depth, size), bf16),
-            pltpu.VMEM((group, tops, depth, size), bf16),
-            dma((2,)),
-            dma((group, tops)),
-            dma((group, tops)),
-            dma((group, tops)),
-            dma((group, tops)),
-        ],
-        compiler_params=pltpu.CompilerParams(
-            collective_id=2, has_side_effects=True, vmem_limit_bytes=32 * 2**20
-        ),
-        name="top",
-    )(sol, blocks, rhs_turned, inverse, chain)
-    return jnp.transpose(stacked, (1, 3, 0, 2)).reshape(tops, size, width)
+    )(rhs_in, slot[None, :], place_rows, leaf_inverse, blocks, mask, rhs, inverse, *top_arrays)
+    solved = jnp.transpose(stacked, (1, 3, 0, 2)).reshape(tops, size, top_width)
+    return leaf, one, solved
 
 
 def shards(
@@ -539,7 +573,7 @@
     top_inverse,
     top_chain,
 ):
-    leaf_solution, solution_one = lower_levels(
+    leaf_solution, solution_one, top_solution = all_levels(
         rhs_in,
         rhs_target,
         leaf_inverse,
@@ -547,8 +581,11 @@
         level_one_pattern[0, 0, 0],
         level_one_rhs[0, 0],
         level_one_inverse[0, 0],
+        top_blocks[0, 0],
+        top_rhs,
+        top_inverse,
+        top_chain,
     )
-    top_solution = top_stage(solution_one, top_blocks[0, 0], top_rhs, top_inverse, top_chain)
     return (leaf_solution, solution_one[None, None], top_solution)
 
 

time: 149 us -> 134 us (0.90)
  local copies, waits for them, and re-layouts: 12.9 us -> 5.83 us
  Pallas kernels: 131 us -> 124 us
    unnamed x18 -> x9, local copies, waits for them, and re-layouts: 10.8 us -> 3.34 us
    pallas_call x2 -> x1, Pallas kernels: 131 us -> 124 us  [all_levels(): pl.pallas_call(functools.partial(lower_kernel, sizes, order), out_shape=(...]
where the time goes in v3:
time: 134 us
  Pallas kernels  124 us (93%)
  local copies, waits for them, and re-layouts  5.83 us (4%)
  other arithmetic  3.62 us (3%)
    pallas_call x1, Pallas kernels, all_levels(): pl.pallas_call(functools.partial(lower_kernel, sizes, order), out_shape=(...  124 us
    unnamed x9, local copies, waits for them, and re-layouts  3.34 us

profile of v3, /device:TPU:17, one launch (start us, length us, event | category | flops | bytes accessed | tf_op | source)
XLA Modules:
  0.0 134.2 jit_solution(11671023165446874445)
XLA Ops:
  0.7 0.7 convert_bitcast_fusion
  1.3 0.1 copy.18
  1.5 0.7 add_select_fusion.1
  2.1 0.4 convert_reduce_fusion
  2.6 0.7 add_select_fusion
  3.3 0.0 copy-start.2
  3.3 0.5 select_reduce_fusion
  3.8 0.1 tile.10
  3.9 0.1 tile.12
  4.0 0.6 broadcast_select_fusion.place_ref
  4.6 0.7 broadcast_in_dim.44.pattern_ref
  5.3 0.0 copy-done.2
  5.3 124.1 %lower.1 = (bf16[1024,1024]{1,0:T(8,128)(2,1)}, bf16[512,256]{1,0:T(8,128)(2,1)}, bf16[8,4,32,512]{3,2,1,0:T(8,128)(2,1)}) custom-call(bf16[1024,1024]{1,0:T(8,128)(2,1)} %rhs_ref.1, s32[1,1024]{1,0:T(1,128)} %bitcast.17, s32[32,1,128]{2,1,0:T(1,128)} %broadcast_select_fusion.place_ref, bf16[2,512,512]{2,1,0:T(8,128)(2,1)} %inverse_ref.1, ...), custom_call_target="tpu_custom_call" | custom-call | tf_op jit(solution)/shard_map/lower/pallas_call | solution.py:509
  129.4 0.0 copy-start
  129.4 0.0 copy-start.1
  129.4 1.4 %copy.19 = bf16[4,512,8,32]{1,3,2,0:T(8,128)(2,1)S(1)} copy(bf16[4,512,8,32]{1,3,0,2:T(8,128)(2,1)} %bitcast.13) | data formatting | bytes 2097152 | tf_op jit(solution)/shard_map/transpose | solution.py:559
  130.9 1.3 copy.20
  132.2 0.0 copy-done
  132.2 1.3 copy.23
  133.5 0.0 copy-done.1
  133.5 0.7 copy.24
  (2 shorter events, 0.0 us)
Async XLA Ops:
  3.3 2.1 %copy-start.2 = (s32[1024]{0:T(1024)}, s32[1024]{0:T(1024)S(1)}, u32[]{:S(2)}) copy-start(s32[1024]{0:T(1024)S(1)} %get-tuple-element.16) | copy-start | bytes 12292
  129.4 2.8 %copy-start = (bf16[1024,1024]{1,0:T(8,128)(2,1)S(1)}, bf16[1024,1024]{1,0:T(8,128)(2,1)}, u32[]{:S(2)}) copy-start(bf16[1024,1024]{1,0:T(8,128)(2,1)} %get-tuple-element.20) | copy-start | bytes 6291460
  129.4 4.1 %copy-start.1 = (bf16[512,256]{1,0:T(8,128)(2,1)S(1)}, bf16[512,256]{1,0:T(8,128)(2,1)}, u32[]{:S(2)}) copy-start(bf16[512,256]{1,0:T(8,128)(2,1)} %get-tuple-element.7) | copy-start | bytes 786436

commit v4 on v3

--- a/solution.py
+++ b/solution.py
@@ -58,7 +58,7 @@
     chain_hbm,
     leaf_ref,
     one_ref,
-    top_ref,
+    turned_ref,
     perm,
     fold,
     sorted_rows,
@@ -81,6 +81,7 @@
     mate_terms,
     summed,
     sums,
+    top_ref,
     load_sems,
     top_load_sems,
     block_sems,
@@ -449,6 +450,8 @@
     for top in range(tops):
         for step in range(pairs):
             on_copy(top, pair_at(step), 1 - side).wait_recv()
+        turned_ref[top] = top_ref[:, top].reshape(2 * pairs * depth, size).T
+    for top in range(tops):
         for step in range(pairs):
             on_copy(top, pair_at(step), side).wait_send()
             if step:
@@ -487,8 +490,8 @@
     bf16 = jnp.bfloat16
     order = sorted(range(cols), key=lambda part: -abs(2 * part - (cols - 1)))
 
-    destination = target // height
-    place = target % height
+    destination = lax.div(target, jnp.int32(height))
+    place = lax.rem(target, jnp.int32(height))
     index = jnp.arange(height, dtype=jnp.int32)
     same = (destination[:, None] == destination[None, :]) & (index[:, None] < index[None, :])
     slot = destination * share + jnp.sum(same.astype(jnp.int32), axis=0)
@@ -506,12 +509,12 @@
     tops, _, top_width = top_arrays[1].shape
     pairs = grids * rows // 2
     depth = top_width // (2 * pairs)
-    leaf, one, stacked = pl.pallas_call(
+    return pl.pallas_call(
         functools.partial(lower_kernel, sizes, order),
         out_shape=(
             jax.ShapeDtypeStruct((height, width), bf16),
             jax.ShapeDtypeStruct(rhs.shape, bf16),
-            jax.ShapeDtypeStruct((2 * pairs, tops, depth, size), bf16),
+            jax.ShapeDtypeStruct((tops, size, top_width), bf16),
         ),
         in_specs=[VMEM, VMEM, VMEM, VMEM, ANY, VMEM, VMEM, VMEM, ANY, ANY, ANY, ANY],
         out_specs=(VMEM, VMEM, VMEM),
@@ -535,6 +538,7 @@
             pltpu.VMEM((tops, pairs, depth, size), bf16),
             pltpu.VMEM((tops, pairs, depth, size), bf16),
             pltpu.VMEM((tops, pairs, depth, size), bf16),
+            pltpu.VMEM((2 * pairs, tops, depth, size), bf16),
             dma((rows,)),
             dma((len(top_arrays),)),
             dma((2, rows)),
@@ -556,8 +560,6 @@
         ),
         name="lower",
     )(rhs_in, slot[None, :], place_rows, leaf_inverse, blocks, mask, rhs, inverse, *top_arrays)
-    solved = jnp.transpose(stacked, (1, 3, 0, 2)).reshape(tops, size, top_width)
-    return leaf, one, solved
 
 
 def shards(

time: 134 us -> 135 us (level)
    unnamed x9, local copies, waits for them, and re-layouts: 3.34 us -> 4.87 us
    transpose x1 -> x0, local copies, waits for them, and re-layouts: 1.45 us -> none  [all_levels(): solved = jnp.transpose(stacked, (1, 3, 0, 2)).reshape(tops, size, top_width)]
    select_n x2 -> x0, other arithmetic: 1.4 us -> none  [the longest x1 0.7 us: all_levels(): place = target % height]
where the time goes in v4:
time: 135 us; the launch traced here: 134 us
  Pallas kernels  124 us (92%)
  local copies, waits for them, and re-layouts  5.9 us (4%)
  other arithmetic  3.62 us (3%)
    pallas_call x1, Pallas kernels, all_levels(): pl.pallas_call(functools.partial(lower_kernel, sizes, order), out_shape=(...  124 us
    unnamed x9, local copies, waits for them, and re-layouts  4.87 us

profile of v4, /device:TPU:17, one launch (start us, length us, event | category | flops | bytes accessed | tf_op | source)
XLA Modules:
  0.0 134.4 jit_solution(1878502328787867088)
XLA Ops:
  0.7 0.7 convert_bitcast_fusion
  1.3 0.1 copy.15
  1.5 0.7 negate_select_fusion.1
  2.1 0.4 convert_reduce_fusion
  2.6 0.7 negate_select_fusion
  3.3 0.0 copy-start.2
  3.3 0.5 select_reduce_fusion
  3.8 0.1 tile.10
  3.9 0.1 tile.12
  4.0 0.6 broadcast_select_fusion.place_ref
  4.6 0.7 broadcast_in_dim.44.pattern_ref
  5.3 0.0 copy-done.2
  5.3 124.2 %lower.1 = (bf16[1024,1024]{1,0:T(8,128)(2,1)}, bf16[512,256]{1,0:T(8,128)(2,1)}, bf16[4,512,256]{2,1,0:T(8,128)(2,1)}) custom-call(bf16[1024,1024]{1,0:T(8,128)(2,1)} %rhs_ref.1, s32[1,1024]{1,0:T(1,128)} %bitcast.13, s32[32,1,128]{2,1,0:T(1,128)} %broadcast_select_fusion.place_ref, bf16[2,512,512]{2,1,0:T(8,128)(2,1)} %inverse_ref.1, ...), custom_call_target="tpu_custom_call" | custom-call | tf_op jit(solution)/shard_map/lower/pallas_call | solution.py:512
  129.6 0.0 copy-start.1
  129.6 0.0 copy-start
  129.6 3.2 %copy.19 = bf16[1024,1024]{1,0:T(8,128)(2,1)} copy(bf16[1024,1024]{1,0:T(8,128)(2,1)} %get-tuple-element.14) | data formatting | bytes 4194304
  132.8 0.0 copy-done.1
  132.8 0.7 copy.20
  133.5 0.0 copy-done
  133.5 1.0 copy.21
  (2 shorter events, 0.0 us)
Async XLA Ops:
  3.3 2.1 %copy-start.2 = (s32[1024]{0:T(1024)}, s32[1024]{0:T(1024)S(1)}, u32[]{:S(2)}) copy-start(s32[1024]{0:T(1024)S(1)} %get-tuple-element.10) | copy-start | bytes 12292
  129.6 3.2 %copy-start.1 = (bf16[512,256]{1,0:T(8,128)(2,1)S(1)}, bf16[512,256]{1,0:T(8,128)(2,1)}, u32[]{:S(2)}) copy-start(bf16[512,256]{1,0:T(8,128)(2,1)} %get-tuple-element.7) | copy-start | bytes 786436
  129.6 3.9 %copy-start = (bf16[4,512,256]{2,1,0:T(8,128)(2,1)S(1)}, bf16[4,512,256]{2,1,0:T(8,128)(2,1)}, u32[]{:S(2)}) copy-start(bf16[4,512,256]{2,1,0:T(8,128)(2,1)} %get-tuple-element.16) | copy-start | bytes 3145732
